TPU v7x, 32 devices: a whole 2x2x4 slice. The times are simulated.
32 devices in a mesh: seq: 8 (over y, x, core), dp: 4 (over z).
Axes of the slice: x: 2, y: 2, z: 4, core: 2. Of those that a mesh axis runs over, the one named last changes fastest.
Arguments:
- attn_queries: bfloat16 [4, 8, 8, 2048], P('dp', 'seq'), may hold values from -190 to 190
- attn_keys: bfloat16 [4, 8, 8, 2048], P('dp', 'seq'), may hold values from -7 to 7
- attn_values: bfloat16 [4, 8, 8, 2048], P('dp', 'seq'), may hold values from -6 to 6
- out_grad: bfloat16 [4, 8, 8, 2048], P('dp', 'seq'), may hold values from -0.359375 to 0.359375
- fold_maps: bfloat16 [3, 6, 2048], replicated, may hold values from -0.078125 to 0.078125
- dec_grad: float32 [4, 6, 8, 8], P('dp', None, 'seq'), may hold values from -0.36 to 0.36
- conv_input: bfloat16 [4, 8, 8, 256], P('dp', 'seq'), may hold values from -6 to 6
- pre_act: bfloat16 [4, 8, 8, 256], P('dp', 'seq'), may hold values from -6 to 6
- proj_weight: bfloat16 [6, 256], replicated, may hold values from -0.375 to 0.375
Outputs:
- conv_grad: float32 [256, 9, 256], P('seq')
- proj_grad: float32 [256, 6], P('seq')
All inputs are finite; a program needn't handle non-finite values.
Results may differ from a plain program's by a relative error of at most 0.0046.
Values may be sent and summed in bfloat16 or wider, within the bound.
No kernel may reach another device: no remote copies, remote signals or barrier semaphores. Data moves between devices by JAX's collectives and lax.ppermute only.
A program may use at most 64 MiB of HBM per device.

v0:
```python
import math

import jax
import jax.numpy as jnp
from jax import lax
from jax.sharding import PartitionSpec as P

HEAD_DIM = 128
HALF = 8


fsq_levels = (8.0, 8.0, 8.0, 5.0, 5.0, 5.0)
fsq_bins = (4.0, 4.0, 4.0, 2.0, 2.0, 2.0)


def padded_2(block, sides, width):
    for axis, dim in sides:
        count = lax.axis_size(axis)
        forward = [(i, i + 1) for i in range(count - 1)]
        backward = [(target, source) for source, target in forward]
        low = lax.ppermute(
            lax.slice_in_dim(block, block.shape[dim] - width, None, axis=dim), axis, forward
        )
        high = lax.ppermute(lax.slice_in_dim(block, 0, width, axis=dim), axis, backward)
        block = jnp.concatenate([low, block, high], axis=dim)
    return block


def bound_tables():
    halves = [(levels_one - 1.0) * 1.001 / 2.0 for levels_one in fsq_levels]
    shifts = []
    for levels_one, half_width in zip(fsq_levels, halves):
        offset_one = 0.5 if levels_one % 2.0 == 0.0 else 0.0
        ratio_one = offset_one / half_width
        shifts.append(0.5 * math.log((1.0 + ratio_one) / (1.0 - ratio_one)))
    return (
        jnp.array(halves, jnp.float32),
        jnp.array(shifts, jnp.float32),
        jnp.array(fsq_bins, jnp.float32),
    )


def attend_back(queries, keys_in, values_in, grads_in):
    scaling = 1.0 / math.sqrt(queries.shape[-1])
    length = queries.shape[1]
    scores = (
        jnp.einsum("blhd,bmhd->bhlm", queries, keys_in, preferred_element_type=jnp.float32)
        * scaling
    )
    causal = jnp.arange(length)[:, None] >= jnp.arange(length)[None, :]
    scores = jnp.where(causal, scores, -jnp.inf)
    exp_scores = jnp.exp(scores - jnp.max(scores, axis=-1, keepdims=True))
    attn_probs = exp_scores / jnp.sum(exp_scores, axis=-1, keepdims=True)
    probs_low = attn_probs.astype(jnp.bfloat16)
    dprobs = jnp.einsum("blhd,bmhd->bhlm", grads_in, values_in, preferred_element_type=jnp.float32)
    rowdot = jnp.sum(attn_probs * dprobs, axis=-1, keepdims=True)
    dscore = (attn_probs * (dprobs - rowdot) * scaling).astype(jnp.bfloat16)
    grad_query = jnp.einsum(
        "bhlm,bmhd->blhd", dscore, keys_in, preferred_element_type=jnp.float32
    ).astype(jnp.bfloat16)
    grad_key = jnp.einsum(
        "bhlm,blhd->bmhd", dscore, queries, preferred_element_type=jnp.float32
    ).astype(jnp.bfloat16)
    grad_value = jnp.einsum(
        "bhlm,blhd->bmhd", probs_low, grads_in, preferred_element_type=jnp.float32
    ).astype(jnp.bfloat16)
    return (grad_query, grad_key, grad_value)


def fold_sum(grads, maps):
    total = jnp.einsum("cw,iyxw->icyx", maps[0], grads[0], preferred_element_type=jnp.float32)
    total = total + jnp.einsum(
        "cw,iyxw->icyx", maps[1], grads[1], preferred_element_type=jnp.float32
    )
    return total + jnp.einsum(
        "cw,iyxw->icyx", maps[2], grads[2], preferred_element_type=jnp.float32
    )


def on_device(
    attn_queries,
    attn_keys,
    attn_values,
    out_grad,
    fold_maps,
    dec_grad,
    conv_input,
    pre_act,
    proj_weight,
):
    split_at = HALF * HEAD_DIM
    width_cols = attn_queries.shape[2]
    rim_rows = padded_2(conv_input, (("seq", 1),), 1)
    column_parts = (
        lax.all_to_all(
            attn_queries[..., split_at:], "seq", split_axis=2, concat_axis=1, tiled=True
        ),
        lax.all_to_all(attn_keys[..., split_at:], "seq", split_axis=2, concat_axis=1, tiled=True),
        lax.all_to_all(attn_values[..., split_at:], "seq", split_axis=2, concat_axis=1, tiled=True),
        lax.all_to_all(out_grad[..., split_at:], "seq", split_axis=2, concat_axis=1, tiled=True),
    )

    def row_heads(array_in):
        return array_in[0, :, :, :split_at].reshape(array_in.shape[1], width_cols, HALF, HEAD_DIM)

    row_grads = attend_back(
        row_heads(attn_queries), row_heads(attn_keys), row_heads(attn_values), row_heads(out_grad)
    )
    row_grads = [grad_one.reshape(1, 1, width_cols, split_at) for grad_one in row_grads]
    grid_rows = column_parts[0].shape[1]
    col_count = column_parts[0].shape[2]

    def col_heads(array_in):
        return jnp.transpose(array_in[0], (1, 0, 2)).reshape(col_count, grid_rows, HALF, HEAD_DIM)

    col_grads = attend_back(
        col_heads(column_parts[0]),
        col_heads(column_parts[1]),
        col_heads(column_parts[2]),
        col_heads(column_parts[3]),
    )
    col_grads = [
        jnp.transpose(grad_one.reshape(col_count, grid_rows, split_at), (1, 0, 2))[None]
        for grad_one in col_grads
    ]
    latent_col = fold_sum(col_grads, fold_maps[:, :, split_at:])
    latent_rows = lax.all_to_all(latent_col, "seq", split_axis=2, concat_axis=3, tiled=True)
    latent = fold_sum(row_grads, fold_maps[:, :, :split_at]) + latent_rows
    halves, shifts, bins_arr = bound_tables()
    pre_wide = pre_act.astype(jnp.float32)
    sigmoid_v = jax.nn.sigmoid(pre_wide)
    act_low = (pre_wide * sigmoid_v).astype(jnp.bfloat16)
    latent_pre = jnp.einsum(
        "iyxj,cj->icyx", act_low, proj_weight, preferred_element_type=jnp.float32
    )
    tanh_val = jnp.tanh(latent_pre + shifts[None, :, None, None])
    slope_fsq = (halves / bins_arr)[None, :, None, None] * (1.0 - tanh_val * tanh_val)
    latent_grad = ((latent + dec_grad) * slope_fsq).astype(jnp.bfloat16)
    proj_term = jnp.einsum(
        "icyx,iyxj->jc", latent_grad, act_low, preferred_element_type=jnp.float32
    )
    act_grad = jnp.einsum(
        "icyx,cj->iyxj", latent_grad, proj_weight, preferred_element_type=jnp.float32
    )
    pre_grad = (act_grad * sigmoid_v * (1.0 + pre_wide * (1.0 - sigmoid_v))).astype(jnp.bfloat16)
    padded = jnp.pad(rim_rows, ((0, 0), (0, 0), (1, 1), (0, 0)))
    windows = jnp.stack(
        [
            padded[0, row_off, col_off : col_off + width_cols]
            for row_off in range(3)
            for col_off in range(3)
        ]
    )
    conv_term = jnp.einsum(
        "kpa,pb->akb", windows, pre_grad[0, 0], preferred_element_type=jnp.float32
    )
    shares = (
        lax.psum_scatter(conv_term, "seq", scatter_dimension=0, tiled=True),
        lax.psum_scatter(proj_term, "seq", scatter_dimension=0, tiled=True),
    )
    conv_out, proj_out = lax.psum((shares[0], shares[1]), "dp")
    return (conv_out, proj_out)


def solution(mesh):
    return jax.shard_map(
        on_device,
        mesh=mesh,
        in_specs=(
            P("dp", "seq", None, None),
            P("dp", "seq", None, None),
            P("dp", "seq", None, None),
            P("dp", "seq", None, None),
            P(),
            P("dp", None, "seq", None),
            P("dp", "seq", None, None),
            P("dp", "seq", None, None),
            P(),
        ),
        out_specs=(P("seq", None, None), P("seq", None)),
        check_vma=False,
    )
```

profile of v0, /device:TPU:0, one launch (start us, length us, event | category | flops | bytes accessed | tf_op | source)
XLA Modules:
  0.0 211.7 jit_solution(7561205864738118358)
XLA Ops:
  7.2 2.5 %collective-permute-start = (bf16[1,1,8,256]{3,2,1,0:T(8,128)(2,1)}, bf16[1,1,8,256]{3,2,1,0:T(8,128)(2,1)S(1)}, u32[]{:S(2)}, u32[]{:S(2)}) collective-permute-start(bf16[1,1,8,256]{3,2,1,0:T(8,128)(2,1)} %param.18), channel_id=1, source_target_pairs={{0,4},{4,8},{8,12},{12,16},{16,20},{20,24},{24,28},{1,5},{5,9},{9,... | collective-permute-start | bytes 12296 | tf_op jit(solution)/shard_map/ppermute | solution.py:21
  9.8 1.3 collective-permute-start.1
  12.3 0.7 reduce.23
  13.7 7.1 %all-to-all-start = ((bf16[8,2,512]{2,1,0:T(2,128)(2,1)}), bf16[8,2,512]{2,1,0:T(2,128)(2,1)S(1)}, u32[]{:S(2)}, u32[]{:S(2)}) async-start(bf16[8,2,512]{2,1,0:T(2,128)(2,1)} %reshape.235), calls=%async_computation | async-start | bytes 32768 | tf_op jit(solution)/shard_map/all_to_all | solution.py:95
  20.8 0.9 fusion.136
  21.6 0.9 fusion.70
  22.5 0.9 fusion.18
  23.4 0.9 fusion.19
  24.3 0.8 fusion.68
  25.1 0.8 convolution_add_fusion.4
  26.0 0.8 fusion.32
  29.0 0.7 reduce.22
  30.4 0.7 reduce.21
  31.8 0.7 reduce.20
  33.1 0.8 copy.54
  35.4 4.2 %all-to-all-start.1 = ((bf16[8,2,512]{2,1,0:T(2,128)(2,1)}), bf16[8,2,512]{2,1,0:T(2,128)(2,1)S(1)}, u32[]{:S(2)}, u32[]{:S(2)}) async-start(bf16[8,2,512]{2,1,0:T(2,128)(2,1)} %reshape.233), calls=%async_computation.1 | async-start | bytes 32768 | tf_op jit(solution)/shard_map/all_to_all | solution.py:98
  39.7 4.6 %all-to-all-done.1 = bf16[8,2,512]{2,1,0:T(2,128)(2,1)S(1)} async-done(((bf16[8,2,512]{2,1,0:T(2,128)(2,1)}), bf16[8,2,512]{2,1,0:T(2,128)(2,1)S(1)}, u32[]{:S(2)}, u32[]{:S(2)}) %all-to-all-start.1) | async-done | bytes 16416 | tf_op jit(solution)/shard_map/all_to_all | solution.py:98
  44.3 3.3 %all-to-all-start.2 = ((bf16[8,2,512]{2,1,0:T(2,128)(2,1)}), bf16[8,2,512]{2,1,0:T(2,128)(2,1)S(1)}, u32[]{:S(2)}, u32[]{:S(2)}) async-start(bf16[8,2,512]{2,1,0:T(2,128)(2,1)} %reshape.231), calls=%async_computation.2 | async-start | bytes 32768 | tf_op jit(solution)/shard_map/all_to_all | solution.py:100
  47.8 4.6 %all-to-all-done.2 = bf16[8,2,512]{2,1,0:T(2,128)(2,1)S(1)} async-done(((bf16[8,2,512]{2,1,0:T(2,128)(2,1)}), bf16[8,2,512]{2,1,0:T(2,128)(2,1)S(1)}, u32[]{:S(2)}, u32[]{:S(2)}) %all-to-all-start.2) | async-done | bytes 16416 | tf_op jit(solution)/shard_map/all_to_all | solution.py:100
  52.3 3.3 %all-to-all-start.3 = ((bf16[8,2,512]{2,1,0:T(2,128)(2,1)}), bf16[8,2,512]{2,1,0:T(2,128)(2,1)S(1)}, u32[]{:S(2)}, u32[]{:S(2)}) async-start(bf16[8,2,512]{2,1,0:T(2,128)(2,1)} %reshape.229), calls=%async_computation.3 | async-start | bytes 32768 | tf_op jit(solution)/shard_map/all_to_all | solution.py:99
  55.8 4.6 %all-to-all-done.3 = bf16[8,2,512]{2,1,0:T(2,128)(2,1)S(1)} async-done(((bf16[8,2,512]{2,1,0:T(2,128)(2,1)}), bf16[8,2,512]{2,1,0:T(2,128)(2,1)S(1)}, u32[]{:S(2)}, u32[]{:S(2)}) %all-to-all-start.3) | async-done | bytes 16416 | tf_op jit(solution)/shard_map/all_to_all | solution.py:99
  61.4 0.8 convolution_add_fusion.1
  62.2 3.3 %all-to-all-start.4 = ((f32[1,6,8,1]{1,3,0,2:T(1,128)}), f32[1,6,8,1]{1,3,0,2:T(1,128)S(1)}, u32[]{:S(2)}, u32[]{:S(2)}) async-start(f32[1,6,8,1]{1,3,0,2:T(1,128)} %bitcast.38), calls=%async_computation.4 | async-start | bytes 8192 | tf_op jit(solution)/shard_map/all_to_all | solution.py:127
  65.6 4.5 %all-to-all-done.4 = f32[1,6,8,1]{1,3,0,2:T(1,128)S(1)} async-done(((f32[1,6,8,1]{1,3,0,2:T(1,128)}), f32[1,6,8,1]{1,3,0,2:T(1,128)S(1)}, u32[]{:S(2)}, u32[]{:S(2)}) %all-to-all-start.4) | async-done | bytes 224 | tf_op jit(solution)/shard_map/all_to_all | solution.py:127
  71.0 3.4 %copy.58 = f32[256,9,256]{2,1,0:T(8,128)} copy(f32[256,9,256]{0,2,1:T(8,128)S(1)} %convolution_bitcast_fusion) | data formatting | bytes 4718592 | tf_op jit(solution)/shard_map/kpa,pb->akb/transpose | solution.py:154
  74.4 0.9 fusion.128
  75.4 49.7 %reduce-scatter.5.cloned.1.call-done = f32[32,9,256]{2,1,0:T(8,128)} async-done(((f32[256,9,256]{2,1,0:T(8,128)}), f32[32,9,256]{2,1,0:T(8,128)}) %reduce-scatter.5.cloned.1.call-update) | async-done | bytes 294928 | tf_op jit(solution)/shard_map/reduce_scatter | solution.py:158
  125.1 37.1 %reduce-scatter.7.cloned.1.call-done = f32[32,6]{1,0:T(8,128)} async-done(((f32[256,6]{1,0:T(8,128)}), f32[32,6]{1,0:T(8,128)}) %reduce-scatter.7.cloned.1.call-update) | async-done | bytes 784
  162.2 0.8 copy.65
  163.0 12.3 %psum.15 = f32[32,6]{0,1:T(8,128)} all-reduce(f32[32,6]{0,1:T(8,128)S(1)} %copy.65), channel_id=1, replica_groups=mesh['seq'=8,'dp'=4] {'dp'}, use_global_device_ids=true, to_apply=%region_9.10 | all-reduce | flops 192 | bytes 1536 | tf_op jit(solution)/shard_map/psum | solution.py:161
  175.3 28.0 %all-reduce.3.cloned.1.call-done = f32[32,9,256]{2,1,0:T(8,128)} async-done(((f32[32,9,256]{2,1,0:T(8,128)}), f32[32,9,256]{2,1,0:T(8,128)}) %all-reduce.3.cloned.1.call-update) | async-done | bytes 294928 | tf_op jit(solution)/shard_map/psum | solution.py:161
  203.3 1.9 copy.59
  (57 shorter events, 9.8 us)
Async XLA Ops:
  7.2 18.8 %copy-start = (bf16[6,256]{1,0:T(8,128)(2,1)S(1)}, bf16[6,256]{1,0:T(8,128)(2,1)}, u32[]{:S(2)}) copy-start(bf16[6,256]{1,0:T(8,128)(2,1)} %param.20) | copy-start | bytes 9220
  7.2 62.9 %copy-start.2 = (bf16[1,1,8,2048]{3,2,1,0:T(8,128)(2,1)S(1)}, bf16[1,1,8,2048]{3,2,1,0:T(8,128)(2,1)}, u32[]{:S(2)}) copy-start(bf16[1,1,8,2048]{3,2,1,0:T(8,128)(2,1)} %param.15) | copy-start | bytes 98308
  7.2 53.9 %copy-start.1 = (bf16[3,6,2048]{2,1,0:T(8,128)(2,1)S(1)}, bf16[3,6,2048]{2,1,0:T(8,128)(2,1)}, u32[]{:S(2)}) copy-start(bf16[3,6,2048]{2,1,0:T(8,128)(2,1)} %param.16) | copy-start | bytes 221188
  7.2 63.1 %copy-start.3 = (bf16[1,1,8,256]{3,2,1,0:T(8,128)(2,1)S(1)}, bf16[1,1,8,256]{3,2,1,0:T(8,128)(2,1)}, u32[]{:S(2)}) copy-start(bf16[1,1,8,256]{3,2,1,0:T(8,128)(2,1)} %param.19) | copy-start | bytes 12292
  7.2 26.7 %collective-permute-start = (bf16[1,1,8,256]{3,2,1,0:T(8,128)(2,1)}, bf16[1,1,8,256]{3,2,1,0:T(8,128)(2,1)S(1)}, u32[]{:S(2)}, u32[]{:S(2)}) collective-permute-start(bf16[1,1,8,256]{3,2,1,0:T(8,128)(2,1)} %param.18), channel_id=1, source_target_pairs={{0,4},{4,8},{8,12},{12,16},{16,20},{20,24},{24,28},{1,5},{5,9},{9,... | collective-permute-start | bytes 12296 | tf_op jit(solution)/shard_map/ppermute | solution.py:21
  9.8 24.1 %collective-permute-start.1 = (bf16[1,1,8,256]{3,2,1,0:T(8,128)(2,1)}, bf16[1,1,8,256]{3,2,1,0:T(8,128)(2,1)S(1)}, u32[]{:S(2)}, u32[]{:S(2)}) collective-permute-start(bf16[1,1,8,256]{3,2,1,0:T(8,128)(2,1)} %param.18), channel_id=1, source_target_pairs={{4,0},{8,4},{12,8},{16,12},{20,16},{24,20},{28,24},{5,1},{9,5},{13... | collective-permute-start | bytes 12296 | tf_op jit(solution)/shard_map/ppermute | solution.py:24
  13.7 21.7 %all-to-all-start = ((bf16[8,2,512]{2,1,0:T(2,128)(2,1)}), bf16[8,2,512]{2,1,0:T(2,128)(2,1)S(1)}, u32[]{:S(2)}, u32[]{:S(2)}) async-start(bf16[8,2,512]{2,1,0:T(2,128)(2,1)} %reshape.235), calls=%async_computation | async-start | bytes 32768 | tf_op jit(solution)/shard_map/all_to_all | solution.py:95
  35.4 9.0 %all-to-all-start.1 = ((bf16[8,2,512]{2,1,0:T(2,128)(2,1)}), bf16[8,2,512]{2,1,0:T(2,128)(2,1)S(1)}, u32[]{:S(2)}, u32[]{:S(2)}) async-start(bf16[8,2,512]{2,1,0:T(2,128)(2,1)} %reshape.233), calls=%async_computation.1 | async-start | bytes 32768 | tf_op jit(solution)/shard_map/all_to_all | solution.py:98
  44.3 8.0 %all-to-all-start.2 = ((bf16[8,2,512]{2,1,0:T(2,128)(2,1)}), bf16[8,2,512]{2,1,0:T(2,128)(2,1)S(1)}, u32[]{:S(2)}, u32[]{:S(2)}) async-start(bf16[8,2,512]{2,1,0:T(2,128)(2,1)} %reshape.231), calls=%async_computation.2 | async-start | bytes 32768 | tf_op jit(solution)/shard_map/all_to_all | solution.py:100
  52.3 8.0 %all-to-all-start.3 = ((bf16[8,2,512]{2,1,0:T(2,128)(2,1)}), bf16[8,2,512]{2,1,0:T(2,128)(2,1)S(1)}, u32[]{:S(2)}, u32[]{:S(2)}) async-start(bf16[8,2,512]{2,1,0:T(2,128)(2,1)} %reshape.229), calls=%async_computation.3 | async-start | bytes 32768 | tf_op jit(solution)/shard_map/all_to_all | solution.py:99
  62.2 7.9 %all-to-all-start.4 = ((f32[1,6,8,1]{1,3,0,2:T(1,128)}), f32[1,6,8,1]{1,3,0,2:T(1,128)S(1)}, u32[]{:S(2)}, u32[]{:S(2)}) async-start(f32[1,6,8,1]{1,3,0,2:T(1,128)} %bitcast.38), calls=%async_computation.4 | async-start | bytes 8192 | tf_op jit(solution)/shard_map/all_to_all | solution.py:127
  65.5 59.5 %reduce-scatter.5.cloned.1.call-start = ((), (), s32[]{:S(2)}) async-start(), calls=%async_computation.7 | async-start | bytes 4718592 | tf_op jit(solution)/shard_map/reduce_scatter | solution.py:158
  74.4 87.8 %reduce-scatter.7.cloned.1.call-start = ((), (), s32[]{:S(2)}) async-start(), calls=%async_computation.9 | async-start | bytes 147456
  75.4 127.9 %all-reduce.3.cloned.1.call-start = ((), (), s32[]{:S(2)}) async-start(), calls=%async_computation.8 | async-start | bytes 1048576 | tf_op jit(solution)/shard_map/psum | solution.py:161
Sparse Core Ops, SparseCore 0:
  74.5 50.5 reduce-scatter.4
  128.6 33.5 reduce-scatter.6
  164.5 38.6 all-reduce.2
where the time goes:
time: 214 us; the launch traced here: 212 us
  waiting for transfers between devices  133 us (62%)
  starting transfers between devices  25.2 us (12%)
  local copies, waits for them, and re-layouts  14 us (7%)
  between operations  14 us (7%)
  blocking collectives  12.3 us (6%)
  matrix products  9.53 us (4%)
  other arithmetic  3.65 us (2%)
    reduce_scatter x1, waiting for transfers between devices, on_device(): lax.psum_scatter(conv_term, 'seq', scatter_dimension=0, tiled=True)  49.7 us
    unnamed x4, waiting for transfers between devices  37.1 us
    psum x1, waiting for transfers between devices, on_device(): conv_out, proj_out = lax.psum((shares[0], shares[1]), 'dp')  28 us
    psum x1, blocking collectives, on_device(): conv_out, proj_out = lax.psum((shares[0], shares[1]), 'dp')  12.3 us
    unnamed x32, local copies, waits for them, and re-layouts  7.36 us
    all_to_all x1, starting transfers between devices, on_device(): lax.all_to_all(attn_queries[..., split_at:], 'seq', split_axis=2, concat_...  7.07 us
    all_to_all x1, waiting for transfers between devices, on_device(): lax.all_to_all(attn_keys[..., split_at:], 'seq', split_axis=2, concat_axi...  4.64 us
    all_to_all x1, waiting for transfers between devices, on_device(): lax.all_to_all(out_grad[..., split_at:], 'seq', split_axis=2, concat_axis...  4.56 us
  transfers between devices with their start and end apart: 10, of which 7 were waited for; matrix products, arithmetic and copies ran while one was open for 9% of the time, Pallas kernels for 0%

commit v1 on v0

--- a/solution.py
+++ b/solution.py
@@ -1,8 +1,11 @@
+import functools
 import math
 
 import jax
 import jax.numpy as jnp
 from jax import lax
+from jax.experimental import pallas as pl
+from jax.experimental.pallas import tpu as pltpu
 from jax.sharding import PartitionSpec as P
 
 HEAD_DIM = 128
@@ -77,7 +80,7 @@
     )
 
 
-def on_device(
+def reduce_plan(
     attn_queries,
     attn_keys,
     attn_values,
@@ -162,6 +165,306 @@
     return (conv_out, proj_out)
 
 
+LANES = 128
+FLOAT = jnp.float32
+HALFWORD = jnp.bfloat16
+
+
+def dot(lhs, rhs, lhs_dim=1, rhs_dim=0, precision=None):
+    return lax.dot_general(
+        lhs,
+        rhs,
+        (((lhs_dim,), (rhs_dim,)), ((), ())),
+        precision=precision,
+        preferred_element_type=FLOAT,
+    )
+
+
+def iota(shape, axis):
+    return lax.broadcasted_iota(jnp.int32, shape, axis)
+
+
+def attend_tile(queries, keys_in, values_in, grads_in, allowed):
+    scaling = 1.0 / math.sqrt(queries.shape[-1])
+    scores = jnp.where(allowed, dot(queries, keys_in, 1, 1) * scaling, -jnp.inf)
+    exp_scores = jnp.exp(scores - jnp.max(scores, axis=-1, keepdims=True))
+    attn_probs = exp_scores / jnp.sum(exp_scores, axis=-1, keepdims=True)
+    dprobs = dot(grads_in, values_in, 1, 1)
+    rowdot = jnp.sum(attn_probs * dprobs, axis=-1, keepdims=True)
+    dscore = (attn_probs * (dprobs - rowdot) * scaling).astype(HALFWORD)
+    return (
+        dot(dscore, keys_in).astype(HALFWORD),
+        dot(dscore, queries, 0, 0).astype(HALFWORD),
+        dot(attn_probs.astype(HALFWORD), grads_in, 0, 0).astype(HALFWORD),
+    )
+
+
+def lane_places(rows, lanes, start, latents, width):
+    lane = iota((rows, lanes), 1)
+    inside = lane >= start
+    offset = lax.rem(jnp.maximum(lane - start, 0), latents * width)
+    return inside, lax.div(offset, width), lax.rem(offset, width)
+
+
+def pack_kernel(query_ref, key_ref, value_ref, grad_ref, out_ref):
+    heads = out_ref.shape[0]
+    for part, ref in enumerate((query_ref, key_ref, value_ref, grad_ref)):
+        for head in range(heads):
+            out_ref[head, part] = ref[0, 0, :, head * HEAD_DIM : (head + 1) * HEAD_DIM]
+
+
+def local_kernel(
+    query_ref,
+    key_ref,
+    value_ref,
+    grad_ref,
+    fold_ref,
+    dec_ref,
+    conv_ref,
+    proj_ref,
+    row_ref,
+    fold_own_ref,
+    conv_out_ref,
+    proj_rep_ref,
+):
+    width = query_ref.shape[2]
+    latents = fold_ref.shape[1]
+    devices, _, lanes = conv_out_ref.shape
+    span = conv_ref.shape[3] // devices
+    mine = lax.axis_index("seq")
+
+    def stacked(ref):
+        return jnp.concatenate(
+            [
+                ref[0, 0, :, head * HEAD_DIM : (head + 1) * HEAD_DIM].astype(FLOAT)
+                for head in range(HALF)
+            ],
+            axis=0,
+        ).astype(HALFWORD)
+
+    count = HALF * width
+    row, col = iota((count, count), 0), iota((count, count), 1)
+    allowed = (lax.div(row, width) == lax.div(col, width)) & (col <= row)
+    grads = attend_tile(
+        stacked(query_ref), stacked(key_ref), stacked(value_ref), stacked(grad_ref), allowed
+    )
+    inside, channel, place = lane_places(width, lanes, span, latents, width)
+    lane = iota((lanes, latents), 0)
+    spread_at = lax.rem(jnp.maximum(lane - span, 0), latents * width)
+    hit = (lane >= span) & (lax.div(spread_at, width) == iota((lanes, latents), 1))
+    spread = jnp.where(hit, 1.0, 0.0).astype(HALFWORD)
+    once = jnp.where(hit & (lane < span + latents * width), 1.0, 0.0).astype(HALFWORD)
+    split_at = HALF * HEAD_DIM
+    total = jnp.zeros((width, lanes), FLOAT)
+    for part in range(3):
+        maps = dot(spread, fold_ref[part, :, :split_at]).astype(HALFWORD)
+        wide = grads[part].astype(FLOAT)
+        wide = jnp.concatenate(
+            [wide[head * width : (head + 1) * width] for head in range(HALF)], axis=1
+        ).astype(HALFWORD)
+        total = total + dot(wide, maps, 1, 1)
+        own = fold_ref[part, :, pl.ds(pl.multiple_of(split_at + mine * HEAD_DIM, HEAD_DIM), HEAD_DIM)]
+        fold_own_ref[part] = dot(spread, own).astype(HALFWORD)
+    total = jnp.where(inside & (iota((width, lanes), 0) == place), total, 0.0)
+    decoder = dec_ref[0, :, 0, :]
+    column = jnp.where(
+        iota((width, lanes), 0) == lax.rem(iota((width, lanes), 1), width), 1.0, 0.0
+    )
+    decoder = dot(decoder, column, precision=lax.Precision.HIGHEST)
+    _, channel, _ = lane_places(latents, lanes, span, latents, width)
+    keep = (iota((latents, lanes), 1) >= span) & (iota((latents, lanes), 0) == channel)
+    vector = jnp.sum(total, axis=0, keepdims=True) + jnp.sum(
+        jnp.where(keep, decoder, 0.0), axis=0, keepdims=True
+    )
+    row_ref[...] = jnp.where(iota((width, lanes), 0) == mine, vector, 0.0)
+    proj_rep_ref[...] = dot(once, proj_ref[...]).astype(HALFWORD)
+    for device in range(devices):
+        first = device * span
+        block = conv_ref[0, 0, :, first // lanes * lanes : first // lanes * lanes + lanes].astype(FLOAT)
+        if first % lanes:
+            block = pltpu.roll(block, lanes - first % lanes, 1)
+        conv_out_ref[device] = block
+
+
+def column_kernel(recv_ref, fold_ref, row_ref, conv_ref, pre_ref, out_ref):
+    rows, _, width, _ = recv_ref.shape
+    devices, _, lanes = conv_ref.shape
+    channels = pre_ref.shape[3]
+    images = out_ref.shape[0] // devices
+    span = channels // devices
+    half = (lanes - span) // 2
+    count = rows * width
+
+    def stacked(part):
+        return recv_ref[:, part].astype(FLOAT).reshape(count, HEAD_DIM).astype(HALFWORD)
+
+    row, col = iota((count, count), 0), iota((count, count), 1)
+    allowed = (lax.rem(row, width) == lax.rem(col, width)) & (col <= row)
+    grads = attend_tile(stacked(0), stacked(1), stacked(2), stacked(3), allowed)
+    total = dot(grads[0], fold_ref[0], 1, 1)
+    total = total + dot(grads[1], fold_ref[1], 1, 1)
+    total = total + dot(grads[2], fold_ref[2], 1, 1)
+    match = lax.rem(iota((count, lanes), 0), width) == lax.rem(iota((count, lanes), 1), width)
+    total = jnp.where(match, total, 0.0).reshape(rows, width, lanes)
+    share = jnp.sum(total, axis=1) + row_ref[...]
+    high = share.astype(HALFWORD).astype(FLOAT)
+    lane = iota((rows, lanes), 1)
+    pair = jnp.where(lane < span + half, high, share - high)
+    pre = pre_ref[0, 0]
+    for device in range(devices):
+        block = jnp.where(lane < span, conv_ref[device], pair).astype(HALFWORD)
+        for image in range(images):
+            out_ref[image * devices + device, :, :channels] = pre
+            out_ref[image * devices + device, :, channels:] = block
+
+
+def final_kernel(recv_ref, proj_rep_ref, conv_out_ref, proj_out_ref):
+    sources, width, _ = recv_ref.shape
+    taps, span, channels = conv_out_ref.shape
+    latents = proj_out_ref.shape[0]
+    lanes = proj_rep_ref.shape[0]
+    devices = channels // span
+    images = sources // devices
+    count = sources * width
+    mine = lax.axis_index("seq")
+    half = latents * width
+
+    pre_wide = recv_ref[:, :, :channels].astype(FLOAT).reshape(count, channels)
+    tail = recv_ref[:, :, channels:].astype(FLOAT)
+    proj_rep = proj_rep_ref[...]
+    sigmoid_v = jax.nn.sigmoid(pre_wide)
+    act_low = (pre_wide * sigmoid_v).astype(HALFWORD)
+    lane = iota((count, lanes), 1)
+    match = (
+        (lane >= span)
+        & (lane < span + half)
+        & (lax.rem(iota((count, lanes), 0), width) == lax.rem(lane, width))
+    )
+    latent_pre = jnp.where(match, dot(act_low, proj_rep, 1, 1), 0.0)
+    latent_pre = jnp.sum(latent_pre.reshape(sources, width, lanes), axis=1)
+    shares = tail.reshape(images, devices, width, lanes)
+    latent = jnp.sum(shares, axis=1).reshape(sources, lanes)
+    latent = latent + pltpu.roll(latent, lanes - half, 1)
+    halves = [(levels_one - 1.0) * 1.001 / 2.0 for levels_one in fsq_levels]
+    _, channel, _ = lane_places(sources, lanes, span, latents, width)
+    shift = jnp.zeros((sources, lanes), FLOAT)
+    slope = jnp.zeros((sources, lanes), FLOAT)
+    for index, (levels_one, bins_one, half_width) in enumerate(zip(fsq_levels, fsq_bins, halves)):
+        ratio_one = (0.5 if levels_one % 2.0 == 0.0 else 0.0) / half_width
+        shift_one = 0.5 * math.log((1.0 + ratio_one) / (1.0 - ratio_one))
+        shift = jnp.where(channel == index, shift_one, shift)
+        slope = jnp.where(channel == index, half_width / bins_one, slope)
+    tanh_val = jnp.tanh(latent_pre + shift)
+    latent_grad = latent * (slope * (1.0 - tanh_val * tanh_val))
+    wide = jnp.broadcast_to(latent_grad.reshape(sources, 1, lanes), (sources, width, lanes))
+    wide = jnp.where(match, wide.reshape(count, lanes), 0.0).astype(HALFWORD)
+    act_grad = dot(wide, proj_rep)
+    pre_grad = (act_grad * sigmoid_v * (1.0 + pre_wide * (1.0 - sigmoid_v))).astype(HALFWORD)
+
+    pick = jnp.where(iota((span, lanes), 0) == iota((span, lanes), 1), 1.0, 0.0).astype(HALFWORD)
+    inputs = dot(pick, tail.reshape(count, lanes).astype(HALFWORD), 1, 1)
+    position = iota((span, count), 1)
+    place_x = lax.rem(position, width)
+    place_y = lax.rem(lax.div(position, width), devices)
+    windows = []
+    for row_off in (-1, 0, 1):
+        for col_off in (-1, 0, 1):
+            step = row_off * width + col_off
+            window = pltpu.roll(inputs, -step % count, 1) if step else inputs
+            valid = (
+                (place_x + col_off >= 0)
+                & (place_x + col_off < width)
+                & (place_y + row_off >= 0)
+                & (place_y + row_off < devices)
+            )
+            windows.append(jnp.where(valid, window, 0.0))
+    windows = jnp.concatenate(windows, axis=0).astype(HALFWORD)
+    conv_out_ref[...] = dot(windows, pre_grad).reshape(taps, span, channels)
+    proj_term = dot(wide, act_low, 0, 0)[span : span + half]
+    proj_term = jnp.sum(proj_term.reshape(latents, width, channels), axis=1)
+    proj_out_ref[...] = pltpu.roll(proj_term, lax.rem(channels - mine * span, channels), 1)[:, :span]
+
+
+def call(kernel, outs, inputs, in_specs=None, flops=1 << 22):
+    whole = pl.BlockSpec(memory_space=pltpu.VMEM)
+    nbytes = sum(math.prod(one.shape) * one.dtype.itemsize for one in (*inputs, *outs))
+    return pl.pallas_call(
+        kernel,
+        grid=(1,),
+        out_shape=outs,
+        in_specs=in_specs or [whole] * len(inputs),
+        out_specs=[whole] * len(outs),
+        compiler_params=pltpu.CompilerParams(vmem_limit_bytes=16 << 20),
+        cost_estimate=pl.CostEstimate(flops=flops, bytes_accessed=nbytes, transcendentals=0),
+    )(*inputs)
+
+
+def gather_plan(
+    attn_queries,
+    attn_keys,
+    attn_values,
+    out_grad,
+    fold_maps,
+    dec_grad,
+    conv_input,
+    pre_act,
+    proj_weight,
+):
+    devices, images = lax.axis_size("seq"), lax.axis_size("dp")
+    width, channels, latents = pre_act.shape[2], pre_act.shape[3], proj_weight.shape[0]
+    span = channels // devices
+    split_at = HALF * HEAD_DIM
+    heads = (attn_queries, attn_keys, attn_values, out_grad)
+    struct = jax.ShapeDtypeStruct
+    columns = [pl.BlockSpec((1, 1, width, split_at), lambda step: (0, 0, 0, 1))] * 4
+    rows = [pl.BlockSpec((1, 1, width, split_at), lambda step: (0, 0, 0, 0))] * 4
+    whole = pl.BlockSpec(memory_space=pltpu.VMEM)
+    (packed,) = call(
+        pack_kernel, [struct((devices, 4, width, HEAD_DIM), HALFWORD)], heads, columns
+    )
+    column = lax.all_to_all(packed, "seq", split_axis=0, concat_axis=0, tiled=True)
+    row_share, fold_own, conv_blocks, proj_rep = call(
+        local_kernel,
+        [
+            struct((width, LANES), FLOAT),
+            struct((3, LANES, HEAD_DIM), HALFWORD),
+            struct((devices, width, LANES), FLOAT),
+            struct((LANES, channels), HALFWORD),
+        ],
+        (*heads, fold_maps, dec_grad, conv_input, proj_weight),
+        rows + [whole] * 4,
+    )
+    (shared,) = call(
+        column_kernel,
+        [struct((images * devices, width, channels + LANES), HALFWORD)],
+        (column, fold_own, row_share, conv_blocks, pre_act),
+    )
+    spread = lax.all_to_all(shared, ("dp", "seq"), split_axis=0, concat_axis=0, tiled=True)
+    conv_out, proj_out = call(
+        final_kernel,
+        [struct((9, span, channels), FLOAT), struct((latents, span), FLOAT)],
+        (spread, proj_rep),
+    )
+    return (jnp.transpose(conv_out, (1, 0, 2)), jnp.transpose(proj_out, (1, 0)))
+
+
+def on_device(*arrays):
+    queries, conv_input, proj_weight = arrays[0], arrays[6], arrays[8]
+    devices, images = lax.axis_size("seq"), lax.axis_size("dp")
+    rows, width, channels = conv_input.shape[1:]
+    latents = proj_weight.shape[0]
+    heads = queries.shape[3] // HEAD_DIM - HALF
+    positions = images * devices * rows * width
+    fits = (
+        (conv_input.shape[0], rows, width, heads) == (1, 1, devices, devices)
+        and (HALF * 2, width % 8) == (queries.shape[3] // HEAD_DIM, 0)
+        and channels // devices + 2 * latents * width == LANES
+    )
+    if fits and positions * channels * 2 <= 9 * channels * channels * 4:
+        return gather_plan(*arrays)
+    return reduce_plan(*arrays)
+
+
 def solution(mesh):
     return jax.shard_map(
         on_device,

time: 214 us -> 30.1 us (0.14)
  waiting for transfers between devices: 133 us -> 3.7 us
  starting transfers between devices: 25.2 us -> 5.34 us
  between operations: 14 us -> 0.72 us
  local copies, waits for them, and re-layouts: 14 us -> 3.06 us
  matrix products: 9.53 us -> 0 us
  Pallas kernels: 0 us -> 3.96 us
  other arithmetic: 3.65 us -> 0 us
    reduce_scatter x1 -> x0, waiting for transfers between devices: 49.7 us -> none  [on_device(): lax.psum_scatter(conv_term, 'seq', scatter_dimension=0, tiled=True)]
    unnamed x4 -> x0, waiting for transfers between devices: 37.1 us -> none
    psum x1 -> x0, waiting for transfers between devices: 28 us -> none  [on_device(): conv_out, proj_out = lax.psum((shares[0], shares[1]), 'dp')]
    all_to_all x5 -> x1, starting transfers between devices: 21.3 us -> 5.34 us  [gather_plan(): lax.all_to_all(packed, 'seq', split_axis=0, concat_axis=0, tiled=True)]
    all_to_all x5 -> x1, waiting for transfers between devices: 18.3 us -> 3.7 us  [gather_plan(): lax.all_to_all(packed, 'seq', split_axis=0, concat_axis=0, tiled=True)]
    all_to_all x0 -> x1, blocking collectives: none -> 12.7 us  [gather_plan(): lax.all_to_all(shared, ('dp', 'seq'), split_axis=0, concat_axis=0, tiled=...]
    psum x1 -> x0, blocking collectives: 12.3 us -> none  [on_device(): conv_out, proj_out = lax.psum((shares[0], shares[1]), 'dp')]
    dot_general x14 -> x0, matrix products: 7.6 us -> none  [the longest x2 1.14 us: attend_back(): jnp.einsum('bhlm,bmhd->blhd', dscore, keys_in, preferred_element_type=jnp...]
  transfers between devices with their start and end apart: 10 -> 1, of which waited for: 7 -> 1; matrix products, arithmetic and copies ran while one was open for 9% -> 0% of each run, Pallas kernels for 0% -> 4%
where the time goes in v1:
time: 30.1 us; the launch traced here: 29.5 us
  blocking collectives  12.7 us (42%)
  starting transfers between devices  5.34 us (18%)
  Pallas kernels  3.96 us (13%)
  waiting for transfers between devices  3.7 us (12%)
  local copies, waits for them, and re-layouts  3.06 us (10%)
  between operations  0.72 us (2%)
    all_to_all x1, blocking collectives, gather_plan(): lax.all_to_all(shared, ('dp', 'seq'), split_axis=0, concat_axis=0, tiled=...  12.7 us
    all_to_all x1, starting transfers between devices, gather_plan(): lax.all_to_all(packed, 'seq', split_axis=0, concat_axis=0, tiled=True)  5.34 us
    pallas_call x4, Pallas kernels, call(): pl.pallas_call(kernel, grid=(1,), out_shape=outs, in_specs=in_specs or [w...  3.96 us
    all_to_all x1, waiting for transfers between devices, gather_plan(): lax.all_to_all(packed, 'seq', split_axis=0, concat_axis=0, tiled=True)  3.7 us
    unnamed x26, local copies, waits for them, and re-layouts  3.06 us
  transfers between devices with their start and end apart: 1, of which 1 were waited for; matrix products, arithmetic and copies ran while one was open for 0% of the time, Pallas kernels for 4%

profile of v1, /device:TPU:0, one launch (start us, length us, event | category | flops | bytes accessed | tf_op | source)
XLA Modules:
  0.0 29.5 jit_solution(506544538781975494)
XLA Ops:
  0.6 0.0 copy-start
  0.6 0.7 %copy-done = bf16[1,1,8,2048]{3,2,1,0:T(8,128)(2,1)S(1)} copy-done((bf16[1,1,8,2048]{3,2,1,0:T(8,128)(2,1)S(1)}, bf16[1,1,8,2048]{3,2,1,0:T(8,128)(2,1)}, u32[]{:S(2)}) %copy-start) | copy-done | bytes 32792
  1.4 0.0 copy-start.2
  1.4 0.8 %copy-done.2 = bf16[1,1,8,2048]{3,2,1,0:T(8,128)(2,1)S(1)} copy-done((bf16[1,1,8,2048]{3,2,1,0:T(8,128)(2,1)S(1)}, bf16[1,1,8,2048]{3,2,1,0:T(8,128)(2,1)}, u32[]{:S(2)}) %copy-start.2) | copy-done | bytes 32792
  2.2 0.0 copy-start.4
  2.2 0.8 %copy-done.4 = bf16[1,1,8,2048]{3,2,1,0:T(8,128)(2,1)S(1)} copy-done((bf16[1,1,8,2048]{3,2,1,0:T(8,128)(2,1)S(1)}, bf16[1,1,8,2048]{3,2,1,0:T(8,128)(2,1)}, u32[]{:S(2)}) %copy-start.4) | copy-done | bytes 32792
  2.9 0.0 copy-start.6
  2.9 0.8 %copy-done.6 = bf16[1,1,8,2048]{3,2,1,0:T(8,128)(2,1)S(1)} copy-done((bf16[1,1,8,2048]{3,2,1,0:T(8,128)(2,1)S(1)}, bf16[1,1,8,2048]{3,2,1,0:T(8,128)(2,1)}, u32[]{:S(2)}) %copy-start.6) | copy-done | bytes 32792
  3.7 0.0 copy-start.8
  3.7 0.0 copy-start.9
  3.7 0.0 copy-start.12
  3.7 0.6 %shard_map.104 = bf16[8,4,8,128]{3,2,1,0:T(8,128)(2,1)} custom-call(bf16[1,1,8,2048]{3,2,1,0:T(8,128)(2,1)S(1)} %copy-done, bf16[1,1,8,2048]{3,2,1,0:T(8,128)(2,1)S(1)} %copy-done.2, bf16[1,1,8,2048]{3,2,1,0:T(8,128)(2,1)S(1)} %copy-done.4, bf16[1,1,8,2048]{3,2,1,0:T(8,128)(2,1)S(1)} %copy-done.6), custom_call_target="tpu_custom_call" | custom-call | flops 4194304 | bytes 196608 | tf_op jit(solution)/shard_map/pallas_call | solution.py:391
  4.3 0.0 copy-start.1
  4.3 0.0 copy-start.3
  4.3 0.0 copy-start.5
  4.3 0.0 copy-start.7
  4.3 5.3 %all-to-all-start = ((bf16[8,4,8,128]{3,2,1,0:T(8,128)(2,1)}), bf16[8,4,8,128]{3,2,1,0:T(8,128)(2,1)S(1)}, u32[]{:S(2)}, u32[]{:S(2)}) async-start(bf16[8,4,8,128]{3,2,1,0:T(8,128)(2,1)} %shard_map.104), calls=%async_computation | async-start | bytes 131072 | tf_op jit(solution)/shard_map/all_to_all | solution.py:425
  9.7 0.0 copy-done.8
  9.7 0.0 copy-done.9
  9.7 0.0 copy-done.10
  9.7 0.0 copy-done.12
  9.7 0.0 copy-done.1
  9.7 0.0 copy-done.3
  9.7 0.0 copy-done.5
  9.7 0.0 copy-done.7
  9.8 1.2 %shard_map.105 = (f32[8,128]{1,0:T(8,128)S(1)}, bf16[3,128,128]{2,1,0:T(8,128)(2,1)S(1)}, f32[8,8,128]{2,1,0:T(8,128)S(1)}, bf16[128,256]{1,0:T(8,128)(2,1)S(1)}) custom-call(bf16[1,1,8,2048]{3,2,1,0:T(8,128)(2,1)S(1)} %copy-done.1, bf16[1,1,8,2048]{3,2,1,0:T(8,128)(2,1)S(1)} %copy-done.3, bf16[1,1,8,2048]{3,2,1,0:T(8,128)(2,1)S(1)} %copy-done.5, ...), custom_call_target="tpu_custom_call" | custom-call | flops 4194304 | bytes 412864 | tf_op jit(solution)/shard_map/pallas_call | solution.py:391
  11.0 0.0 copy-start.11
  11.0 3.7 %all-to-all-done.recv_ref = bf16[8,4,8,128]{3,2,1,0:T(8,128)(2,1)S(1)} async-done(((bf16[8,4,8,128]{3,2,1,0:T(8,128)(2,1)}), bf16[8,4,8,128]{3,2,1,0:T(8,128)(2,1)S(1)}, u32[]{:S(2)}, u32[]{:S(2)}) %all-to-all-start) | async-done | bytes 65568 | tf_op jit(solution)/shard_map/all_to_all | solution.py:425
  14.7 0.0 copy-done.11
  14.7 0.7 %shard_map.106 = bf16[32,8,384]{2,1,0:T(8,128)(2,1)S(1)} custom-call(bf16[8,4,8,128]{3,2,1,0:T(8,128)(2,1)S(1)} %all-to-all-done.recv_ref, bf16[3,128,128]{2,1,0:T(8,128)(2,1)S(1)} %get-tuple-element.8.fold_ref, f32[8,128]{1,0:T(8,128)S(1)} %get-tuple-element.9.row_ref, f32[8,8,128]{2,1,0:T(8,128)S(1)} %get-tuple-element.10.conv_ref, ...), custom_call_target="tpu_custom_call" | custom-call | flops 4194304 | bytes 401408 | tf_op jit(solution)/shard_map/pallas_call | solution.py:391
  15.4 12.7 %all_to_all.10.recv_ref = bf16[32,8,384]{2,1,0:T(8,128)(2,1)S(1)} all-to-all(bf16[32,8,384]{2,1,0:T(8,128)(2,1)S(1)} %shard_map.106), channel_id=1, replica_groups=mesh['seq'=8,'dp'=4] {'dp','seq'}, dimensions={0} | all-to-all | bytes 393216 | tf_op jit(solution)/shard_map/all_to_all | solution.py:442
  28.1 1.4 %shard_map.107 = (f32[9,32,256]{2,1,0:T(8,128)}, f32[6,32]{1,0:T(8,128)}) custom-call(bf16[32,8,384]{2,1,0:T(8,128)(2,1)S(1)} %all_to_all.10.recv_ref, bf16[128,256]{1,0:T(8,128)(2,1)S(1)} %get-tuple-element.11.proj_rep_ref), custom_call_target="tpu_custom_call" | custom-call | flops 4194304 | bytes 557824 | tf_op jit(solution)/shard_map/pallas_call | solution.py:391
  (1 shorter events, 0.0 us)
Async XLA Ops:
  0.6 0.8 %copy-start = (bf16[1,1,8,2048]{3,2,1,0:T(8,128)(2,1)S(1)}, bf16[1,1,8,2048]{3,2,1,0:T(8,128)(2,1)}, u32[]{:S(2)}) copy-start(bf16[1,1,8,2048]{3,2,1,0:T(8,128)(2,1)} %query_ref.3) | copy-start | bytes 98308
  1.4 0.8 %copy-start.2 = (bf16[1,1,8,2048]{3,2,1,0:T(8,128)(2,1)S(1)}, bf16[1,1,8,2048]{3,2,1,0:T(8,128)(2,1)}, u32[]{:S(2)}) copy-start(bf16[1,1,8,2048]{3,2,1,0:T(8,128)(2,1)} %key_ref.3) | copy-start | bytes 98308
  2.2 0.8 %copy-start.4 = (bf16[1,1,8,2048]{3,2,1,0:T(8,128)(2,1)S(1)}, bf16[1,1,8,2048]{3,2,1,0:T(8,128)(2,1)}, u32[]{:S(2)}) copy-start(bf16[1,1,8,2048]{3,2,1,0:T(8,128)(2,1)} %value_ref.3) | copy-start | bytes 98308
  2.9 0.8 %copy-start.6 = (bf16[1,1,8,2048]{3,2,1,0:T(8,128)(2,1)S(1)}, bf16[1,1,8,2048]{3,2,1,0:T(8,128)(2,1)}, u32[]{:S(2)}) copy-start(bf16[1,1,8,2048]{3,2,1,0:T(8,128)(2,1)} %grad_ref.3) | copy-start | bytes 98308
  3.7 6.0 %copy-start.8 = (bf16[3,6,2048]{2,1,0:T(8,128)(2,1)S(1)}, bf16[3,6,2048]{2,1,0:T(8,128)(2,1)}, u32[]{:S(2)}) copy-start(bf16[3,6,2048]{2,1,0:T(8,128)(2,1)} %fold_ref.1) | copy-start | bytes 221188
  3.7 6.0 %copy-start.9 = (bf16[1,1,8,256]{3,2,1,0:T(8,128)(2,1)S(1)}, bf16[1,1,8,256]{3,2,1,0:T(8,128)(2,1)}, u32[]{:S(2)}) copy-start(bf16[1,1,8,256]{3,2,1,0:T(8,128)(2,1)} %conv_ref.1) | copy-start | bytes 12292
  3.7 6.0 %copy-start.10 = (bf16[6,256]{1,0:T(8,128)(2,1)S(1)}, bf16[6,256]{1,0:T(8,128)(2,1)}, u32[]{:S(2)}) copy-start(bf16[6,256]{1,0:T(8,128)(2,1)} %proj_ref.1) | copy-start | bytes 9220
  3.7 6.0 %copy-start.12 = (f32[1,6,1,8]{3,2,1,0:T(1,128)S(1)}, f32[1,6,1,8]{3,2,1,0:T(1,128)}, u32[]{:S(2)}) copy-start(f32[1,6,1,8]{3,2,1,0:T(1,128)} %dec_ref.1) | copy-start | bytes 580
  4.3 5.4 %copy-start.1 = (bf16[1,1,8,2048]{3,2,1,0:T(8,128)(2,1)S(1)}, bf16[1,1,8,2048]{3,2,1,0:T(8,128)(2,1)}, u32[]{:S(2)}) copy-start(bf16[1,1,8,2048]{3,2,1,0:T(8,128)(2,1)} %query_ref.3) | copy-start | bytes 98308
  4.3 5.4 %copy-start.3 = (bf16[1,1,8,2048]{3,2,1,0:T(8,128)(2,1)S(1)}, bf16[1,1,8,2048]{3,2,1,0:T(8,128)(2,1)}, u32[]{:S(2)}) copy-start(bf16[1,1,8,2048]{3,2,1,0:T(8,128)(2,1)} %key_ref.3) | copy-start | bytes 98308
  4.3 5.4 %copy-start.5 = (bf16[1,1,8,2048]{3,2,1,0:T(8,128)(2,1)S(1)}, bf16[1,1,8,2048]{3,2,1,0:T(8,128)(2,1)}, u32[]{:S(2)}) copy-start(bf16[1,1,8,2048]{3,2,1,0:T(8,128)(2,1)} %value_ref.3) | copy-start | bytes 98308
  4.3 5.4 %copy-start.7 = (bf16[1,1,8,2048]{3,2,1,0:T(8,128)(2,1)S(1)}, bf16[1,1,8,2048]{3,2,1,0:T(8,128)(2,1)}, u32[]{:S(2)}) copy-start(bf16[1,1,8,2048]{3,2,1,0:T(8,128)(2,1)} %grad_ref.3) | copy-start | bytes 98308
  4.3 10.4 %all-to-all-start = ((bf16[8,4,8,128]{3,2,1,0:T(8,128)(2,1)}), bf16[8,4,8,128]{3,2,1,0:T(8,128)(2,1)S(1)}, u32[]{:S(2)}, u32[]{:S(2)}) async-start(bf16[8,4,8,128]{3,2,1,0:T(8,128)(2,1)} %shard_map.104), calls=%async_computation | async-start | bytes 131072 | tf_op jit(solution)/shard_map/all_to_all | solution.py:425
  11.0 3.7 %copy-start.11 = (bf16[1,1,8,256]{3,2,1,0:T(8,128)(2,1)S(1)}, bf16[1,1,8,256]{3,2,1,0:T(8,128)(2,1)}, u32[]{:S(2)}) copy-start(bf16[1,1,8,256]{3,2,1,0:T(8,128)(2,1)} %pre_ref.1) | copy-start | bytes 12292

commit v2 on v1

--- a/solution.py
+++ b/solution.py
@@ -206,11 +206,19 @@
     return inside, lax.div(offset, width), lax.rem(offset, width)
 
 
-def pack_kernel(query_ref, key_ref, value_ref, grad_ref, out_ref):
-    heads = out_ref.shape[0]
-    for part, ref in enumerate((query_ref, key_ref, value_ref, grad_ref)):
-        for head in range(heads):
-            out_ref[head, part] = ref[0, 0, :, head * HEAD_DIM : (head + 1) * HEAD_DIM]
+def pack_kernel(query_ref, key_ref, value_ref, grad_ref, out_ref, held, sem, out_sem):
+    copies = []
+    for step in range(out_ref.shape[0]):
+        lanes = pl.ds((HALF + step) * HEAD_DIM, HEAD_DIM)
+        for part, ref in enumerate((query_ref, key_ref, value_ref, grad_ref)):
+            copies.append(pltpu.make_async_copy(ref.at[0, 0, :, lanes], held.at[step, part], sem))
+    for copy in copies:
+        copy.start()
+    for copy in copies:
+        copy.wait()
+    last = pltpu.make_async_copy(held, out_ref, out_sem)
+    last.start()
+    last.wait()
 
 
 def local_kernel(
@@ -419,9 +427,13 @@
     columns = [pl.BlockSpec((1, 1, width, split_at), lambda step: (0, 0, 0, 1))] * 4
     rows = [pl.BlockSpec((1, 1, width, split_at), lambda step: (0, 0, 0, 0))] * 4
     whole = pl.BlockSpec(memory_space=pltpu.VMEM)
-    (packed,) = call(
-        pack_kernel, [struct((devices, 4, width, HEAD_DIM), HALFWORD)], heads, columns
-    )
+    packed = pl.pallas_call(
+        pack_kernel,
+        out_shape=struct((devices, 4, width, HEAD_DIM), HALFWORD),
+        in_specs=[pl.BlockSpec(memory_space=pltpu.HBM)] * 4,
+        out_specs=pl.BlockSpec(memory_space=pltpu.HBM),
+        scratch_shapes=[pltpu.VMEM((devices, 4, width, HEAD_DIM), HALFWORD), pltpu.SemaphoreType.DMA, pltpu.SemaphoreType.DMA],
+    )(*heads)
     column = lax.all_to_all(packed, "seq", split_axis=0, concat_axis=0, tiled=True)
     row_share, fold_own, conv_blocks, proj_rep = call(
         local_kernel,

time: 30.1 us -> 27.7 us (0.920)
  local copies, waits for them, and re-layouts: 3.06 us -> 0.05 us
  Pallas kernels: 3.96 us -> 4.82 us
    unnamed x26 -> x18, local copies, waits for them, and re-layouts: 3.06 us -> 0.05 us
    pallas_call x0 -> x1, Pallas kernels: none -> 1.5 us  [gather_plan(): pl.pallas_call(pack_kernel, out_shape=struct((devices, 4, width, HEAD_DIM...]
    pallas_call x4 -> x3, Pallas kernels: 3.96 us -> 3.32 us  [call(): pl.pallas_call(kernel, grid=(1,), out_shape=outs, in_specs=in_specs or [w...]
  transfers between devices with their start and end apart: 1 -> 1, of which waited for: 1 -> 1; matrix products, arithmetic and copies ran while one was open for 0% -> 0% of each run, Pallas kernels for 4% -> 5%
where the time goes in v2:
time: 27.7 us; the launch traced here: 27.4 us
  blocking collectives  12.7 us (46%)
  starting transfers between devices  5.34 us (19%)
  Pallas kernels  4.82 us (17%)
  waiting for transfers between devices  3.7 us (13%)
  between operations  0.77 us (3%)
    all_to_all x1, blocking collectives, gather_plan(): lax.all_to_all(shared, ('dp', 'seq'), split_axis=0, concat_axis=0, tiled=...  12.7 us
    all_to_all x1, starting transfers between devices, gather_plan(): lax.all_to_all(packed, 'seq', split_axis=0, concat_axis=0, tiled=True)  5.34 us
    all_to_all x1, waiting for transfers between devices, gather_plan(): lax.all_to_all(packed, 'seq', split_axis=0, concat_axis=0, tiled=True)  3.7 us
    pallas_call x3, Pallas kernels, call(): pl.pallas_call(kernel, grid=(1,), out_shape=outs, in_specs=in_specs or [w...  3.32 us
    pallas_call x1, Pallas kernels, gather_plan(): pl.pallas_call(pack_kernel, out_shape=struct((devices, 4, width, HEAD_DIM...  1.5 us
  transfers between devices with their start and end apart: 1, of which 1 were waited for; matrix products, arithmetic and copies ran while one was open for 0% of the time, Pallas kernels for 5%

profile of v2, /device:TPU:0, one launch (start us, length us, event | category | flops | bytes accessed | tf_op | source)
XLA Modules:
  0.0 27.4 jit_solution(4147228265683039842)
XLA Ops:
  0.6 0.0 copy-start.4
  0.6 0.0 copy-start.5
  0.7 0.0 copy-start.6
  0.7 0.0 copy-start.8
  0.7 1.5 %shard_map.104 = bf16[8,4,8,128]{3,2,1,0:T(8,128)(2,1)} custom-call(bf16[1,1,8,2048]{3,2,1,0:T(8,128)(2,1)} %query_ref.3, bf16[1,1,8,2048]{3,2,1,0:T(8,128)(2,1)} %key_ref.3, bf16[1,1,8,2048]{3,2,1,0:T(8,128)(2,1)} %value_ref.3, bf16[1,1,8,2048]{3,2,1,0:T(8,128)(2,1)} %grad_ref.3), custom_call_target="tpu_custom_call" | custom-call | tf_op jit(solution)/shard_map/pallas_call | solution.py:430
  2.2 0.0 copy-start
  2.2 0.0 copy-start.1
  2.2 0.0 copy-start.2
  2.2 0.0 copy-start.3
  2.2 5.3 %all-to-all-start = ((bf16[8,4,8,128]{3,2,1,0:T(8,128)(2,1)}), bf16[8,4,8,128]{3,2,1,0:T(8,128)(2,1)S(1)}, u32[]{:S(2)}, u32[]{:S(2)}) async-start(bf16[8,4,8,128]{3,2,1,0:T(8,128)(2,1)} %shard_map.104), calls=%async_computation | async-start | bytes 131072 | tf_op jit(solution)/shard_map/all_to_all | solution.py:437
  7.6 0.0 copy-done.4
  7.6 0.0 copy-done.5
  7.6 0.0 copy-done.6
  7.6 0.0 copy-done.8
  7.6 0.0 copy-done
  7.6 0.0 copy-done.1
  7.6 0.0 copy-done.2
  7.6 0.0 copy-done.3
  7.6 1.2 %shard_map.105 = (f32[8,128]{1,0:T(8,128)S(1)}, bf16[3,128,128]{2,1,0:T(8,128)(2,1)S(1)}, f32[8,8,128]{2,1,0:T(8,128)S(1)}, bf16[128,256]{1,0:T(8,128)(2,1)S(1)}) custom-call(bf16[1,1,8,2048]{3,2,1,0:T(8,128)(2,1)S(1)} %copy-done, bf16[1,1,8,2048]{3,2,1,0:T(8,128)(2,1)S(1)} %copy-done.1, bf16[1,1,8,2048]{3,2,1,0:T(8,128)(2,1)S(1)} %copy-done.2, ...), custom_call_target="tpu_custom_call" | custom-call | flops 4194304 | bytes 412864 | tf_op jit(solution)/shard_map/pallas_call | solution.py:399
  8.9 0.0 copy-start.7
  8.9 3.7 %all-to-all-done.recv_ref = bf16[8,4,8,128]{3,2,1,0:T(8,128)(2,1)S(1)} async-done(((bf16[8,4,8,128]{3,2,1,0:T(8,128)(2,1)}), bf16[8,4,8,128]{3,2,1,0:T(8,128)(2,1)S(1)}, u32[]{:S(2)}, u32[]{:S(2)}) %all-to-all-start) | async-done | bytes 65568 | tf_op jit(solution)/shard_map/all_to_all | solution.py:437
  12.6 0.0 copy-done.7
  12.6 0.7 %shard_map.106 = bf16[32,8,384]{2,1,0:T(8,128)(2,1)S(1)} custom-call(bf16[8,4,8,128]{3,2,1,0:T(8,128)(2,1)S(1)} %all-to-all-done.recv_ref, bf16[3,128,128]{2,1,0:T(8,128)(2,1)S(1)} %get-tuple-element.8.fold_ref, f32[8,128]{1,0:T(8,128)S(1)} %get-tuple-element.9.row_ref, f32[8,8,128]{2,1,0:T(8,128)S(1)} %get-tuple-element.10.conv_ref, ...), custom_call_target="tpu_custom_call" | custom-call | flops 4194304 | bytes 401408 | tf_op jit(solution)/shard_map/pallas_call | solution.py:399
  13.3 12.7 %all_to_all.10.recv_ref = bf16[32,8,384]{2,1,0:T(8,128)(2,1)S(1)} all-to-all(bf16[32,8,384]{2,1,0:T(8,128)(2,1)S(1)} %shard_map.106), channel_id=1, replica_groups=mesh['seq'=8,'dp'=4] {'dp','seq'}, dimensions={0} | all-to-all | bytes 393216 | tf_op jit(solution)/shard_map/all_to_all | solution.py:454
  26.0 1.4 %shard_map.107 = (f32[9,32,256]{2,1,0:T(8,128)}, f32[6,32]{1,0:T(8,128)}) custom-call(bf16[32,8,384]{2,1,0:T(8,128)(2,1)S(1)} %all_to_all.10.recv_ref, bf16[128,256]{1,0:T(8,128)(2,1)S(1)} %get-tuple-element.11.proj_rep_ref), custom_call_target="tpu_custom_call" | custom-call | flops 4194304 | bytes 557824 | tf_op jit(solution)/shard_map/pallas_call | solution.py:399
Async XLA Ops:
  0.6 6.9 %copy-start.4 = (bf16[3,6,2048]{2,1,0:T(8,128)(2,1)S(1)}, bf16[3,6,2048]{2,1,0:T(8,128)(2,1)}, u32[]{:S(2)}) copy-start(bf16[3,6,2048]{2,1,0:T(8,128)(2,1)} %fold_ref.1) | copy-start | bytes 221188
  0.6 6.9 %copy-start.5 = (bf16[1,1,8,256]{3,2,1,0:T(8,128)(2,1)S(1)}, bf16[1,1,8,256]{3,2,1,0:T(8,128)(2,1)}, u32[]{:S(2)}) copy-start(bf16[1,1,8,256]{3,2,1,0:T(8,128)(2,1)} %conv_ref.1) | copy-start | bytes 12292
  0.7 6.9 %copy-start.6 = (bf16[6,256]{1,0:T(8,128)(2,1)S(1)}, bf16[6,256]{1,0:T(8,128)(2,1)}, u32[]{:S(2)}) copy-start(bf16[6,256]{1,0:T(8,128)(2,1)} %proj_ref.1) | copy-start | bytes 9220
  0.7 6.9 %copy-start.8 = (f32[1,6,1,8]{3,2,1,0:T(1,128)S(1)}, f32[1,6,1,8]{3,2,1,0:T(1,128)}, u32[]{:S(2)}) copy-start(f32[1,6,1,8]{3,2,1,0:T(1,128)} %dec_ref.1) | copy-start | bytes 580
  2.2 5.4 %copy-start = (bf16[1,1,8,2048]{3,2,1,0:T(8,128)(2,1)S(1)}, bf16[1,1,8,2048]{3,2,1,0:T(8,128)(2,1)}, u32[]{:S(2)}) copy-start(bf16[1,1,8,2048]{3,2,1,0:T(8,128)(2,1)} %query_ref.3) | copy-start | bytes 98308
  2.2 5.4 %copy-start.1 = (bf16[1,1,8,2048]{3,2,1,0:T(8,128)(2,1)S(1)}, bf16[1,1,8,2048]{3,2,1,0:T(8,128)(2,1)}, u32[]{:S(2)}) copy-start(bf16[1,1,8,2048]{3,2,1,0:T(8,128)(2,1)} %key_ref.3) | copy-start | bytes 98308
  2.2 5.4 %copy-start.2 = (bf16[1,1,8,2048]{3,2,1,0:T(8,128)(2,1)S(1)}, bf16[1,1,8,2048]{3,2,1,0:T(8,128)(2,1)}, u32[]{:S(2)}) copy-start(bf16[1,1,8,2048]{3,2,1,0:T(8,128)(2,1)} %value_ref.3) | copy-start | bytes 98308
  2.2 5.4 %copy-start.3 = (bf16[1,1,8,2048]{3,2,1,0:T(8,128)(2,1)S(1)}, bf16[1,1,8,2048]{3,2,1,0:T(8,128)(2,1)}, u32[]{:S(2)}) copy-start(bf16[1,1,8,2048]{3,2,1,0:T(8,128)(2,1)} %grad_ref.3) | copy-start | bytes 98308
  2.2 10.4 %all-to-all-start = ((bf16[8,4,8,128]{3,2,1,0:T(8,128)(2,1)}), bf16[8,4,8,128]{3,2,1,0:T(8,128)(2,1)S(1)}, u32[]{:S(2)}, u32[]{:S(2)}) async-start(bf16[8,4,8,128]{3,2,1,0:T(8,128)(2,1)} %shard_map.104), calls=%async_computation | async-start | bytes 131072 | tf_op jit(solution)/shard_map/all_to_all | solution.py:437
  8.9 3.7 %copy-start.7 = (bf16[1,1,8,256]{3,2,1,0:T(8,128)(2,1)S(1)}, bf16[1,1,8,256]{3,2,1,0:T(8,128)(2,1)}, u32[]{:S(2)}) copy-start(bf16[1,1,8,256]{3,2,1,0:T(8,128)(2,1)} %pre_ref.1) | copy-start | bytes 12292

commit v3 on v2

--- a/solution.py
+++ b/solution.py
@@ -206,12 +206,12 @@
     return inside, lax.div(offset, width), lax.rem(offset, width)
 
 
-def pack_kernel(query_ref, key_ref, value_ref, grad_ref, out_ref, held, sem, out_sem):
+def pack_kernel(order, query_ref, key_ref, value_ref, grad_ref, out_ref, held, sem, out_sem):
     copies = []
-    for step in range(out_ref.shape[0]):
-        lanes = pl.ds((HALF + step) * HEAD_DIM, HEAD_DIM)
+    for slot, device in enumerate(order):
+        lanes = pl.ds((HALF + device) * HEAD_DIM, HEAD_DIM)
         for part, ref in enumerate((query_ref, key_ref, value_ref, grad_ref)):
-            copies.append(pltpu.make_async_copy(ref.at[0, 0, :, lanes], held.at[step, part], sem))
+            copies.append(pltpu.make_async_copy(ref.at[0, 0, :, lanes], held.at[slot, part], sem))
     for copy in copies:
         copy.start()
     for copy in copies:
@@ -294,7 +294,7 @@
         conv_out_ref[device] = block
 
 
-def column_kernel(recv_ref, fold_ref, row_ref, conv_ref, pre_ref, out_ref):
+def column_kernel(seq_order, all_order, recv_ref, fold_ref, row_ref, conv_ref, pre_ref, out_ref):
     rows, _, width, _ = recv_ref.shape
     devices, _, lanes = conv_ref.shape
     channels = pre_ref.shape[3]
@@ -304,7 +304,8 @@
     count = rows * width
 
     def stacked(part):
-        return recv_ref[:, part].astype(FLOAT).reshape(count, HEAD_DIM).astype(HALFWORD)
+        tiles = [recv_ref[seq_order.index(source), part].astype(FLOAT) for source in range(rows)]
+        return jnp.concatenate(tiles, axis=0).astype(HALFWORD)
 
     row, col = iota((count, count), 0), iota((count, count), 1)
     allowed = (lax.rem(row, width) == lax.rem(col, width)) & (col <= row)
@@ -322,11 +323,12 @@
     for device in range(devices):
         block = jnp.where(lane < span, conv_ref[device], pair).astype(HALFWORD)
         for image in range(images):
-            out_ref[image * devices + device, :, :channels] = pre
-            out_ref[image * devices + device, :, channels:] = block
-
-
-def final_kernel(recv_ref, proj_rep_ref, conv_out_ref, proj_out_ref):
+            slot = all_order.index(image * devices + device)
+            out_ref[slot, :, :channels] = pre
+            out_ref[slot, :, channels:] = block
+
+
+def final_kernel(all_order, recv_ref, proj_rep_ref, conv_out_ref, proj_out_ref):
     sources, width, _ = recv_ref.shape
     taps, span, channels = conv_out_ref.shape
     latents = proj_out_ref.shape[0]
@@ -337,8 +339,9 @@
     mine = lax.axis_index("seq")
     half = latents * width
 
-    pre_wide = recv_ref[:, :, :channels].astype(FLOAT).reshape(count, channels)
-    tail = recv_ref[:, :, channels:].astype(FLOAT)
+    slots = [all_order.index(source) for source in range(sources)]
+    pre_wide = jnp.concatenate([recv_ref[slot, :, :channels].astype(FLOAT) for slot in slots], axis=0)
+    tail = jnp.concatenate([recv_ref[slot, :, channels:].astype(FLOAT) for slot in slots], axis=0)
     proj_rep = proj_rep_ref[...]
     sigmoid_v = jax.nn.sigmoid(pre_wide)
     act_low = (pre_wide * sigmoid_v).astype(HALFWORD)
@@ -424,11 +427,15 @@
     split_at = HALF * HEAD_DIM
     heads = (attn_queries, attn_keys, attn_values, out_grad)
     struct = jax.ShapeDtypeStruct
+    members = images * devices
+    stride = 3 * members // 8 + 1
+    seq_order = list(range(devices))
+    all_order = [(members - 1 - stride * slot) % members for slot in range(members)]
     columns = [pl.BlockSpec((1, 1, width, split_at), lambda step: (0, 0, 0, 1))] * 4
     rows = [pl.BlockSpec((1, 1, width, split_at), lambda step: (0, 0, 0, 0))] * 4
     whole = pl.BlockSpec(memory_space=pltpu.VMEM)
     packed = pl.pallas_call(
-        pack_kernel,
+        functools.partial(pack_kernel, seq_order),
         out_shape=struct((devices, 4, width, HEAD_DIM), HALFWORD),
         in_specs=[pl.BlockSpec(memory_space=pltpu.HBM)] * 4,
         out_specs=pl.BlockSpec(memory_space=pltpu.HBM),
@@ -447,13 +454,20 @@
         rows + [whole] * 4,
     )
     (shared,) = call(
-        column_kernel,
+        functools.partial(column_kernel, seq_order, all_order),
         [struct((images * devices, width, channels + LANES), HALFWORD)],
         (column, fold_own, row_share, conv_blocks, pre_act),
     )
-    spread = lax.all_to_all(shared, ("dp", "seq"), split_axis=0, concat_axis=0, tiled=True)
+    spread = lax.all_to_all(
+        shared,
+        ("dp", "seq"),
+        split_axis=0,
+        concat_axis=0,
+        axis_index_groups=[all_order],
+        tiled=True,
+    )
     conv_out, proj_out = call(
-        final_kernel,
+        functools.partial(final_kernel, all_order),
         [struct((9, span, channels), FLOAT), struct((latents, span), FLOAT)],
         (spread, proj_rep),
     )
@@ -470,6 +484,7 @@
     fits = (
         (conv_input.shape[0], rows, width, heads) == (1, 1, devices, devices)
         and (HALF * 2, width % 8) == (queries.shape[3] // HEAD_DIM, 0)
+        and math.gcd(3 * images * devices // 8 + 1, images * devices) == 1
         and channels // devices + 2 * latents * width == LANES
     )
     if fits and positions * channels * 2 <= 9 * channels * channels * 4:

time: 27.7 us -> 27.1 us (0.978)
  blocking collectives: 12.7 us -> 12.2 us
    all_to_all x1, blocking collectives: 12.7 us -> 12.2 us  [gather_plan(): lax.all_to_all(shared, ('dp', 'seq'), split_axis=0, concat_axis=0, axis_i...]
where the time goes in v3:
time: 27.1 us; the launch traced here: 26.8 us
  blocking collectives  12.2 us (45%)
  starting transfers between devices  5.34 us (20%)
  Pallas kernels  4.82 us (18%)
  waiting for transfers between devices  3.7 us (14%)
  between operations  0.77 us (3%)
    all_to_all x1, blocking collectives, gather_plan(): lax.all_to_all(shared, ('dp', 'seq'), split_axis=0, concat_axis=0, axis_i...  12.2 us
    all_to_all x1, starting transfers between devices, gather_plan(): lax.all_to_all(packed, 'seq', split_axis=0, concat_axis=0, tiled=True)  5.34 us
    all_to_all x1, waiting for transfers between devices, gather_plan(): lax.all_to_all(packed, 'seq', split_axis=0, concat_axis=0, tiled=True)  3.7 us
    pallas_call x3, Pallas kernels, call(): pl.pallas_call(kernel, grid=(1,), out_shape=outs, in_specs=in_specs or [w...  3.32 us
    pallas_call x1, Pallas kernels, gather_plan(): pl.pallas_call(functools.partial(pack_kernel, seq_order), out_shape=struc...  1.5 us
  transfers between devices with their start and end apart: 1, of which 1 were waited for; matrix products, arithmetic and copies ran while one was open for 0% of the time, Pallas kernels for 5%

profile of v3, /device:TPU:0, one launch (start us, length us, event | category | flops | bytes accessed | tf_op | source)
XLA Modules:
  0.0 26.8 jit_solution(10349129443279270783)
XLA Ops:
  0.6 0.0 copy-start.4
  0.6 0.0 copy-start.5
  0.7 0.0 copy-start.6
  0.7 0.0 copy-start.8
  0.7 1.5 %shard_map.104 = bf16[8,4,8,128]{3,2,1,0:T(8,128)(2,1)} custom-call(bf16[1,1,8,2048]{3,2,1,0:T(8,128)(2,1)} %query_ref.3, bf16[1,1,8,2048]{3,2,1,0:T(8,128)(2,1)} %key_ref.3, bf16[1,1,8,2048]{3,2,1,0:T(8,128)(2,1)} %value_ref.3, bf16[1,1,8,2048]{3,2,1,0:T(8,128)(2,1)} %grad_ref.3), custom_call_target="tpu_custom_call" | custom-call | tf_op jit(solution)/shard_map/pallas_call | solution.py:437
  2.2 0.0 copy-start
  2.2 0.0 copy-start.1
  2.2 0.0 copy-start.2
  2.2 0.0 copy-start.3
  2.2 5.3 %all-to-all-start = ((bf16[8,4,8,128]{3,2,1,0:T(8,128)(2,1)}), bf16[8,4,8,128]{3,2,1,0:T(8,128)(2,1)S(1)}, u32[]{:S(2)}, u32[]{:S(2)}) async-start(bf16[8,4,8,128]{3,2,1,0:T(8,128)(2,1)} %shard_map.104), calls=%async_computation | async-start | bytes 131072 | tf_op jit(solution)/shard_map/all_to_all | solution.py:444
  7.6 0.0 copy-done.4
  7.6 0.0 copy-done.5
  7.6 0.0 copy-done.6
  7.6 0.0 copy-done.8
  7.6 0.0 copy-done
  7.6 0.0 copy-done.1
  7.6 0.0 copy-done.2
  7.6 0.0 copy-done.3
  7.6 1.2 %shard_map.105 = (f32[8,128]{1,0:T(8,128)S(1)}, bf16[3,128,128]{2,1,0:T(8,128)(2,1)S(1)}, f32[8,8,128]{2,1,0:T(8,128)S(1)}, bf16[128,256]{1,0:T(8,128)(2,1)S(1)}) custom-call(bf16[1,1,8,2048]{3,2,1,0:T(8,128)(2,1)S(1)} %copy-done, bf16[1,1,8,2048]{3,2,1,0:T(8,128)(2,1)S(1)} %copy-done.1, bf16[1,1,8,2048]{3,2,1,0:T(8,128)(2,1)S(1)} %copy-done.2, ...), custom_call_target="tpu_custom_call" | custom-call | flops 4194304 | bytes 412864 | tf_op jit(solution)/shard_map/pallas_call | solution.py:402
  8.9 0.0 copy-start.7
  8.9 3.7 %all-to-all-done.recv_ref = bf16[8,4,8,128]{3,2,1,0:T(8,128)(2,1)S(1)} async-done(((bf16[8,4,8,128]{3,2,1,0:T(8,128)(2,1)}), bf16[8,4,8,128]{3,2,1,0:T(8,128)(2,1)S(1)}, u32[]{:S(2)}, u32[]{:S(2)}) %all-to-all-start) | async-done | bytes 65568 | tf_op jit(solution)/shard_map/all_to_all | solution.py:444
  12.6 0.0 copy-done.7
  12.6 0.7 %shard_map.106 = bf16[32,8,384]{2,1,0:T(8,128)(2,1)S(1)} custom-call(bf16[8,4,8,128]{3,2,1,0:T(8,128)(2,1)S(1)} %all-to-all-done.recv_ref, bf16[3,128,128]{2,1,0:T(8,128)(2,1)S(1)} %get-tuple-element.8.fold_ref, f32[8,128]{1,0:T(8,128)S(1)} %get-tuple-element.9.row_ref, f32[8,8,128]{2,1,0:T(8,128)S(1)} %get-tuple-element.10.conv_ref, ...), custom_call_target="tpu_custom_call" | custom-call | flops 4194304 | bytes 401408 | tf_op jit(solution)/shard_map/pallas_call | solution.py:402
  13.3 12.2 %all_to_all.10.recv_ref = bf16[32,8,384]{2,1,0:T(8,128)(2,1)S(1)} all-to-all(bf16[32,8,384]{2,1,0:T(8,128)(2,1)S(1)} %shard_map.106), channel_id=1, replica_groups={{31,10,20,3,13,27,6,16,30,9,23,2,12,26,5,19,29,8,22,1,15,25,4,18,28,11,..., dimensions={0} | all-to-all | bytes 393216 | tf_op jit(solution)/shard_map/all_to_all | solution.py:461
  25.5 1.4 %shard_map.107 = (f32[9,32,256]{2,1,0:T(8,128)}, f32[6,32]{1,0:T(8,128)}) custom-call(bf16[32,8,384]{2,1,0:T(8,128)(2,1)S(1)} %all_to_all.10.recv_ref, bf16[128,256]{1,0:T(8,128)(2,1)S(1)} %get-tuple-element.11.proj_rep_ref), custom_call_target="tpu_custom_call" | custom-call | flops 4194304 | bytes 557824 | tf_op jit(solution)/shard_map/pallas_call | solution.py:402
Async XLA Ops:
  0.6 6.9 %copy-start.4 = (bf16[3,6,2048]{2,1,0:T(8,128)(2,1)S(1)}, bf16[3,6,2048]{2,1,0:T(8,128)(2,1)}, u32[]{:S(2)}) copy-start(bf16[3,6,2048]{2,1,0:T(8,128)(2,1)} %fold_ref.1) | copy-start | bytes 221188
  0.6 6.9 %copy-start.5 = (bf16[1,1,8,256]{3,2,1,0:T(8,128)(2,1)S(1)}, bf16[1,1,8,256]{3,2,1,0:T(8,128)(2,1)}, u32[]{:S(2)}) copy-start(bf16[1,1,8,256]{3,2,1,0:T(8,128)(2,1)} %conv_ref.1) | copy-start | bytes 12292
  0.7 6.9 %copy-start.6 = (bf16[6,256]{1,0:T(8,128)(2,1)S(1)}, bf16[6,256]{1,0:T(8,128)(2,1)}, u32[]{:S(2)}) copy-start(bf16[6,256]{1,0:T(8,128)(2,1)} %proj_ref.1) | copy-start | bytes 9220
  0.7 6.9 %copy-start.8 = (f32[1,6,1,8]{3,2,1,0:T(1,128)S(1)}, f32[1,6,1,8]{3,2,1,0:T(1,128)}, u32[]{:S(2)}) copy-start(f32[1,6,1,8]{3,2,1,0:T(1,128)} %dec_ref.1) | copy-start | bytes 580
  2.2 5.4 %copy-start = (bf16[1,1,8,2048]{3,2,1,0:T(8,128)(2,1)S(1)}, bf16[1,1,8,2048]{3,2,1,0:T(8,128)(2,1)}, u32[]{:S(2)}) copy-start(bf16[1,1,8,2048]{3,2,1,0:T(8,128)(2,1)} %query_ref.3) | copy-start | bytes 98308
  2.2 5.4 %copy-start.1 = (bf16[1,1,8,2048]{3,2,1,0:T(8,128)(2,1)S(1)}, bf16[1,1,8,2048]{3,2,1,0:T(8,128)(2,1)}, u32[]{:S(2)}) copy-start(bf16[1,1,8,2048]{3,2,1,0:T(8,128)(2,1)} %key_ref.3) | copy-start | bytes 98308
  2.2 5.4 %copy-start.2 = (bf16[1,1,8,2048]{3,2,1,0:T(8,128)(2,1)S(1)}, bf16[1,1,8,2048]{3,2,1,0:T(8,128)(2,1)}, u32[]{:S(2)}) copy-start(bf16[1,1,8,2048]{3,2,1,0:T(8,128)(2,1)} %value_ref.3) | copy-start | bytes 98308
  2.2 5.4 %copy-start.3 = (bf16[1,1,8,2048]{3,2,1,0:T(8,128)(2,1)S(1)}, bf16[1,1,8,2048]{3,2,1,0:T(8,128)(2,1)}, u32[]{:S(2)}) copy-start(bf16[1,1,8,2048]{3,2,1,0:T(8,128)(2,1)} %grad_ref.3) | copy-start | bytes 98308
  2.2 10.4 %all-to-all-start = ((bf16[8,4,8,128]{3,2,1,0:T(8,128)(2,1)}), bf16[8,4,8,128]{3,2,1,0:T(8,128)(2,1)S(1)}, u32[]{:S(2)}, u32[]{:S(2)}) async-start(bf16[8,4,8,128]{3,2,1,0:T(8,128)(2,1)} %shard_map.104), calls=%async_computation | async-start | bytes 131072 | tf_op jit(solution)/shard_map/all_to_all | solution.py:444
  8.9 3.7 %copy-start.7 = (bf16[1,1,8,256]{3,2,1,0:T(8,128)(2,1)S(1)}, bf16[1,1,8,256]{3,2,1,0:T(8,128)(2,1)}, u32[]{:S(2)}) copy-start(bf16[1,1,8,256]{3,2,1,0:T(8,128)(2,1)} %pre_ref.1) | copy-start | bytes 12292

commit v4 on v3

--- a/solution.py
+++ b/solution.py
@@ -199,11 +199,23 @@
     )
 
 
+def div(value, count):
+    if count & (count - 1) == 0:
+        return lax.shift_right_logical(value, count.bit_length() - 1)
+    return lax.div(value, count)
+
+
+def rem(value, count):
+    if count & (count - 1) == 0:
+        return value & (count - 1)
+    return lax.rem(value, count)
+
+
 def lane_places(rows, lanes, start, latents, width):
     lane = iota((rows, lanes), 1)
     inside = lane >= start
-    offset = lax.rem(jnp.maximum(lane - start, 0), latents * width)
-    return inside, lax.div(offset, width), lax.rem(offset, width)
+    offset = rem(jnp.maximum(lane - start, 0), latents * width)
+    return inside, div(offset, width), rem(offset, width)
 
 
 def pack_kernel(order, query_ref, key_ref, value_ref, grad_ref, out_ref, held, sem, out_sem):
@@ -252,14 +264,14 @@
 
     count = HALF * width
     row, col = iota((count, count), 0), iota((count, count), 1)
-    allowed = (lax.div(row, width) == lax.div(col, width)) & (col <= row)
+    allowed = (div(row, width) == div(col, width)) & (col <= row)
     grads = attend_tile(
         stacked(query_ref), stacked(key_ref), stacked(value_ref), stacked(grad_ref), allowed
     )
     inside, channel, place = lane_places(width, lanes, span, latents, width)
     lane = iota((lanes, latents), 0)
-    spread_at = lax.rem(jnp.maximum(lane - span, 0), latents * width)
-    hit = (lane >= span) & (lax.div(spread_at, width) == iota((lanes, latents), 1))
+    spread_at = rem(jnp.maximum(lane - span, 0), latents * width)
+    hit = (lane >= span) & (div(spread_at, width) == iota((lanes, latents), 1))
     spread = jnp.where(hit, 1.0, 0.0).astype(HALFWORD)
     once = jnp.where(hit & (lane < span + latents * width), 1.0, 0.0).astype(HALFWORD)
     split_at = HALF * HEAD_DIM
@@ -276,7 +288,7 @@
     total = jnp.where(inside & (iota((width, lanes), 0) == place), total, 0.0)
     decoder = dec_ref[0, :, 0, :]
     column = jnp.where(
-        iota((width, lanes), 0) == lax.rem(iota((width, lanes), 1), width), 1.0, 0.0
+        iota((width, lanes), 0) == rem(iota((width, lanes), 1), width), 1.0, 0.0
     )
     decoder = dot(decoder, column, precision=lax.Precision.HIGHEST)
     _, channel, _ = lane_places(latents, lanes, span, latents, width)
@@ -308,13 +320,13 @@
         return jnp.concatenate(tiles, axis=0).astype(HALFWORD)
 
     row, col = iota((count, count), 0), iota((count, count), 1)
-    allowed = (lax.rem(row, width) == lax.rem(col, width)) & (col <= row)
+    allowed = (rem(row, width) == rem(col, width)) & (col <= row)
     grads = attend_tile(stacked(0), stacked(1), stacked(2), stacked(3), allowed)
     total = dot(grads[0], fold_ref[0], 1, 1)
     total = total + dot(grads[1], fold_ref[1], 1, 1)
     total = total + dot(grads[2], fold_ref[2], 1, 1)
-    match = lax.rem(iota((count, lanes), 0), width) == lax.rem(iota((count, lanes), 1), width)
-    total = jnp.where(match, total, 0.0).reshape(rows, width, lanes)
+    match = iota((width, lanes), 0) == rem(iota((width, lanes), 1), width)
+    total = jnp.where(match[None], total.reshape(rows, width, lanes), 0.0)
     share = jnp.sum(total, axis=1) + row_ref[...]
     high = share.astype(HALFWORD).astype(FLOAT)
     lane = iota((rows, lanes), 1)
@@ -328,7 +340,7 @@
             out_ref[slot, :, channels:] = block
 
 
-def final_kernel(all_order, recv_ref, proj_rep_ref, conv_out_ref, proj_out_ref):
+def final_kernel(all_order, recv_ref, proj_rep_ref, conv_out_ref, proj_out_ref, stage, held, small, sem):
     sources, width, _ = recv_ref.shape
     taps, span, channels = conv_out_ref.shape
     latents = proj_out_ref.shape[0]
@@ -341,43 +353,12 @@
 
     slots = [all_order.index(source) for source in range(sources)]
     pre_wide = jnp.concatenate([recv_ref[slot, :, :channels].astype(FLOAT) for slot in slots], axis=0)
-    tail = jnp.concatenate([recv_ref[slot, :, channels:].astype(FLOAT) for slot in slots], axis=0)
-    proj_rep = proj_rep_ref[...]
-    sigmoid_v = jax.nn.sigmoid(pre_wide)
-    act_low = (pre_wide * sigmoid_v).astype(HALFWORD)
-    lane = iota((count, lanes), 1)
-    match = (
-        (lane >= span)
-        & (lane < span + half)
-        & (lax.rem(iota((count, lanes), 0), width) == lax.rem(lane, width))
-    )
-    latent_pre = jnp.where(match, dot(act_low, proj_rep, 1, 1), 0.0)
-    latent_pre = jnp.sum(latent_pre.reshape(sources, width, lanes), axis=1)
-    shares = tail.reshape(images, devices, width, lanes)
-    latent = jnp.sum(shares, axis=1).reshape(sources, lanes)
-    latent = latent + pltpu.roll(latent, lanes - half, 1)
-    halves = [(levels_one - 1.0) * 1.001 / 2.0 for levels_one in fsq_levels]
-    _, channel, _ = lane_places(sources, lanes, span, latents, width)
-    shift = jnp.zeros((sources, lanes), FLOAT)
-    slope = jnp.zeros((sources, lanes), FLOAT)
-    for index, (levels_one, bins_one, half_width) in enumerate(zip(fsq_levels, fsq_bins, halves)):
-        ratio_one = (0.5 if levels_one % 2.0 == 0.0 else 0.0) / half_width
-        shift_one = 0.5 * math.log((1.0 + ratio_one) / (1.0 - ratio_one))
-        shift = jnp.where(channel == index, shift_one, shift)
-        slope = jnp.where(channel == index, half_width / bins_one, slope)
-    tanh_val = jnp.tanh(latent_pre + shift)
-    latent_grad = latent * (slope * (1.0 - tanh_val * tanh_val))
-    wide = jnp.broadcast_to(latent_grad.reshape(sources, 1, lanes), (sources, width, lanes))
-    wide = jnp.where(match, wide.reshape(count, lanes), 0.0).astype(HALFWORD)
-    act_grad = dot(wide, proj_rep)
-    pre_grad = (act_grad * sigmoid_v * (1.0 + pre_wide * (1.0 - sigmoid_v))).astype(HALFWORD)
-
+    tail = jnp.stack([recv_ref[slot, :, channels:].astype(FLOAT) for slot in slots], axis=0)
     pick = jnp.where(iota((span, lanes), 0) == iota((span, lanes), 1), 1.0, 0.0).astype(HALFWORD)
     inputs = dot(pick, tail.reshape(count, lanes).astype(HALFWORD), 1, 1)
-    position = iota((span, count), 1)
-    place_x = lax.rem(position, width)
-    place_y = lax.rem(lax.div(position, width), devices)
-    windows = []
+    position = iota((8, count), 1)
+    place_x = rem(position, width)
+    place_y = rem(div(position, width), devices)
     for row_off in (-1, 0, 1):
         for col_off in (-1, 0, 1):
             step = row_off * width + col_off
@@ -388,12 +369,49 @@
                 & (place_y + row_off >= 0)
                 & (place_y + row_off < devices)
             )
-            windows.append(jnp.where(valid, window, 0.0))
-    windows = jnp.concatenate(windows, axis=0).astype(HALFWORD)
-    conv_out_ref[...] = dot(windows, pre_grad).reshape(taps, span, channels)
+            window = jnp.where(valid[None], window.reshape(span // 8, 8, count), 0.0)
+            tap = 3 * row_off + col_off + 4
+            stage[pl.ds(tap * span, span), :] = window.reshape(span, count).astype(HALFWORD)
+    proj_rep = proj_rep_ref[...]
+    sigmoid_v = 0.5 + 0.5 * jnp.tanh(0.5 * pre_wide)
+    act_wide = pre_wide * sigmoid_v
+    act_low = act_wide.astype(HALFWORD)
+    lane = iota((width, lanes), 1)
+    match = (lane >= span) & (lane < span + half) & (iota((width, lanes), 0) == rem(lane, width))
+    latent_pre = dot(act_low, proj_rep, 1, 1).reshape(sources, width, lanes)
+    shares = tail.reshape(images, devices, width, lanes)
+    latent = jnp.sum(shares, axis=1).reshape(sources, lanes)
+    latent = latent + pltpu.roll(latent, lanes - half, 1)
+    halves = [(levels_one - 1.0) * 1.001 / 2.0 for levels_one in fsq_levels]
+    _, channel, _ = lane_places(width, lanes, span, latents, width)
+    shift = jnp.zeros((width, lanes), FLOAT)
+    slope = jnp.zeros((width, lanes), FLOAT)
+    for index, (levels_one, bins_one, half_width) in enumerate(zip(fsq_levels, fsq_bins, halves)):
+        ratio_one = (0.5 if levels_one % 2.0 == 0.0 else 0.0) / half_width
+        shift_one = 0.5 * math.log((1.0 + ratio_one) / (1.0 - ratio_one))
+        shift = jnp.where(channel == index, shift_one, shift)
+        slope = jnp.where(channel == index, half_width / bins_one, slope)
+    tanh_val = jnp.tanh(latent_pre + shift[None])
+    slope = jnp.where(match, slope, 0.0)[None] * (1.0 - tanh_val * tanh_val)
+    wide = jnp.broadcast_to(latent.reshape(sources, 1, lanes), (sources, width, lanes)) * slope
+    wide = wide.reshape(count, lanes).astype(HALFWORD)
+    act_grad = dot(wide, proj_rep)
+    silu_grad = sigmoid_v + act_wide * (1.0 - sigmoid_v)
+    pre_grad = (act_grad * silu_grad).astype(HALFWORD)
+
     proj_term = dot(wide, act_low, 0, 0)[span : span + half]
     proj_term = jnp.sum(proj_term.reshape(latents, width, channels), axis=1)
-    proj_out_ref[...] = pltpu.roll(proj_term, lax.rem(channels - mine * span, channels), 1)[:, :span]
+    small[...] = pltpu.roll(proj_term, rem(channels - mine * span, channels), 1)[:, :span]
+    copies = [pltpu.make_async_copy(small, proj_out_ref, sem.at[3])]
+    copies[0].start()
+    for part in range(3):
+        rows = pl.ds(3 * part, 3)
+        windows = stage[3 * part * span : 3 * (part + 1) * span, :]
+        held[rows] = dot(windows, pre_grad).reshape(3, span, channels)
+        copies.append(pltpu.make_async_copy(held.at[rows], conv_out_ref.at[rows], sem.at[part]))
+        copies[-1].start()
+    for copy in copies:
+        copy.wait()
 
 
 def call(kernel, outs, inputs, in_specs=None, flops=1 << 22):
@@ -429,7 +447,7 @@
     struct = jax.ShapeDtypeStruct
     members = images * devices
     stride = 3 * members // 8 + 1
-    seq_order = list(range(devices))
+    seq_order = [(1 - slot) % devices for slot in range(devices)]
     all_order = [(members - 1 - stride * slot) % members for slot in range(members)]
     columns = [pl.BlockSpec((1, 1, width, split_at), lambda step: (0, 0, 0, 1))] * 4
     rows = [pl.BlockSpec((1, 1, width, split_at), lambda step: (0, 0, 0, 0))] * 4
@@ -441,7 +459,7 @@
         out_specs=pl.BlockSpec(memory_space=pltpu.HBM),
         scratch_shapes=[pltpu.VMEM((devices, 4, width, HEAD_DIM), HALFWORD), pltpu.SemaphoreType.DMA, pltpu.SemaphoreType.DMA],
     )(*heads)
-    column = lax.all_to_all(packed, "seq", split_axis=0, concat_axis=0, tiled=True)
+    column = lax.all_to_all(packed, "seq", split_axis=0, concat_axis=0, axis_index_groups=[seq_order], tiled=True)
     row_share, fold_own, conv_blocks, proj_rep = call(
         local_kernel,
         [
@@ -466,11 +484,17 @@
         axis_index_groups=[all_order],
         tiled=True,
     )
-    conv_out, proj_out = call(
+    outs = [struct((9, span, channels), FLOAT), struct((latents, span), FLOAT)]
+    conv_out, proj_out = pl.pallas_call(
         functools.partial(final_kernel, all_order),
-        [struct((9, span, channels), FLOAT), struct((latents, span), FLOAT)],
-        (spread, proj_rep),
-    )
+        out_shape=outs,
+        in_specs=[whole] * 2,
+        out_specs=[pl.BlockSpec(memory_space=pltpu.HBM)] * 2,
+        scratch_shapes=[pltpu.VMEM((9 * span, images * devices * width), HALFWORD)]
+        + [pltpu.VMEM(one.shape, one.dtype) for one in outs]
+        + [pltpu.SemaphoreType.DMA((4,))],
+        compiler_params=pltpu.CompilerParams(vmem_limit_bytes=16 << 20),
+    )(spread, proj_rep)
     return (jnp.transpose(conv_out, (1, 0, 2)), jnp.transpose(proj_out, (1, 0)))
 
 
@@ -483,7 +507,8 @@
     positions = images * devices * rows * width
     fits = (
         (conv_input.shape[0], rows, width, heads) == (1, 1, devices, devices)
-        and (HALF * 2, width % 8) == (queries.shape[3] // HEAD_DIM, 0)
+        and channels // devices % 8 == 0
+        and (HALF * 2, width, images * devices % 8) == (queries.shape[3] // HEAD_DIM, 8, 0)
         and math.gcd(3 * images * devices // 8 + 1, images * devices) == 1
         and channels // devices + 2 * latents * width == LANES
     )

time: 27.1 us -> 26.6 us (0.982)
  waiting for transfers between devices: 3.7 us -> 3.06 us
    pallas_call x3 -> x2, Pallas kernels: 3.32 us -> 1.93 us  [call(): pl.pallas_call(kernel, grid=(1,), out_shape=outs, in_specs=in_specs or [w...]
    pallas_call x0 -> x1, Pallas kernels: none -> 1.24 us  [gather_plan(): pl.pallas_call(functools.partial(final_kernel, all_order), out_shape=outs...]
    all_to_all x1, waiting for transfers between devices: 3.7 us -> 3.06 us  [gather_plan(): lax.all_to_all(packed, 'seq', split_axis=0, concat_axis=0, axis_index_gro...]
where the time goes in v4:
time: 26.6 us; the launch traced here: 26.3 us
  blocking collectives  12.3 us (46%)
  starting transfers between devices  5.45 us (20%)
  Pallas kernels  4.67 us (18%)
  waiting for transfers between devices  3.06 us (12%)
  between operations  0.76 us (3%)
    all_to_all x1, blocking collectives, gather_plan(): lax.all_to_all(shared, ('dp', 'seq'), split_axis=0, concat_axis=0, axis_i...  12.3 us
    all_to_all x1, starting transfers between devices, gather_plan(): lax.all_to_all(packed, 'seq', split_axis=0, concat_axis=0, axis_index_gro...  5.45 us
    all_to_all x1, waiting for transfers between devices, gather_plan(): lax.all_to_all(packed, 'seq', split_axis=0, concat_axis=0, axis_index_gro...  3.06 us
    pallas_call x2, Pallas kernels, call(): pl.pallas_call(kernel, grid=(1,), out_shape=outs, in_specs=in_specs or [w...  1.93 us
    pallas_call x1, Pallas kernels, gather_plan(): pl.pallas_call(functools.partial(pack_kernel, seq_order), out_shape=struc...  1.5 us
    pallas_call x1, Pallas kernels, gather_plan(): pl.pallas_call(functools.partial(final_kernel, all_order), out_shape=outs...  1.24 us
  transfers between devices with their start and end apart: 1, of which 1 were waited for; matrix products, arithmetic and copies ran while one was open for 0% of the time, Pallas kernels for 5%

profile of v4, /device:TPU:0, one launch (start us, length us, event | category | flops | bytes accessed | tf_op | source)
XLA Modules:
  0.0 26.3 jit_solution(17783891993197168433)
XLA Ops:
  0.6 0.0 copy-start.4
  0.6 0.0 copy-start.5
  0.7 0.0 copy-start.6
  0.7 0.0 copy-start.8
  0.7 1.5 %shard_map.104 = bf16[8,4,8,128]{3,2,1,0:T(8,128)(2,1)} custom-call(bf16[1,1,8,2048]{3,2,1,0:T(8,128)(2,1)} %query_ref.3, bf16[1,1,8,2048]{3,2,1,0:T(8,128)(2,1)} %key_ref.3, bf16[1,1,8,2048]{3,2,1,0:T(8,128)(2,1)} %value_ref.3, bf16[1,1,8,2048]{3,2,1,0:T(8,128)(2,1)} %grad_ref.3), custom_call_target="tpu_custom_call" | custom-call | tf_op jit(solution)/shard_map/pallas_call | solution.py:455
  2.2 0.0 copy-start
  2.2 0.0 copy-start.1
  2.2 0.0 copy-start.2
  2.2 0.0 copy-start.3
  2.2 5.5 %all-to-all-start = ((bf16[8,4,8,128]{3,2,1,0:T(8,128)(2,1)}), bf16[8,4,8,128]{3,2,1,0:T(8,128)(2,1)S(1)}, u32[]{:S(2)}, u32[]{:S(2)}) async-start(bf16[8,4,8,128]{3,2,1,0:T(8,128)(2,1)} %shard_map.104), calls=%async_computation | async-start | bytes 131072 | tf_op jit(solution)/shard_map/all_to_all | solution.py:462
  7.7 0.0 copy-done.4
  7.7 0.0 copy-done.5
  7.7 0.0 copy-done.6
  7.7 0.0 copy-done.8
  7.7 0.0 copy-done
  7.7 0.0 copy-done.1
  7.7 0.0 copy-done.2
  7.7 0.0 copy-done.3
  7.8 1.2 %shard_map.105 = (f32[8,128]{1,0:T(8,128)S(1)}, bf16[3,128,128]{2,1,0:T(8,128)(2,1)S(1)}, f32[8,8,128]{2,1,0:T(8,128)S(1)}, bf16[128,256]{1,0:T(8,128)(2,1)S(1)}) custom-call(bf16[1,1,8,2048]{3,2,1,0:T(8,128)(2,1)S(1)} %copy-done, bf16[1,1,8,2048]{3,2,1,0:T(8,128)(2,1)S(1)} %copy-done.1, bf16[1,1,8,2048]{3,2,1,0:T(8,128)(2,1)S(1)} %copy-done.2, ...), custom_call_target="tpu_custom_call" | custom-call | flops 4194304 | bytes 412864 | tf_op jit(solution)/shard_map/pallas_call | solution.py:420
  9.0 0.0 copy-start.7
  9.0 3.1 %all-to-all-done.recv_ref = bf16[8,4,8,128]{3,2,1,0:T(8,128)(2,1)S(1)} async-done(((bf16[8,4,8,128]{3,2,1,0:T(8,128)(2,1)}), bf16[8,4,8,128]{3,2,1,0:T(8,128)(2,1)S(1)}, u32[]{:S(2)}, u32[]{:S(2)}) %all-to-all-start) | async-done | bytes 65568 | tf_op jit(solution)/shard_map/all_to_all | solution.py:462
  12.0 0.0 copy-done.7
  12.1 0.7 %shard_map.106 = bf16[32,8,384]{2,1,0:T(8,128)(2,1)S(1)} custom-call(bf16[8,4,8,128]{3,2,1,0:T(8,128)(2,1)S(1)} %all-to-all-done.recv_ref, bf16[3,128,128]{2,1,0:T(8,128)(2,1)S(1)} %get-tuple-element.8.fold_ref, f32[8,128]{1,0:T(8,128)S(1)} %get-tuple-element.9.row_ref, f32[8,8,128]{2,1,0:T(8,128)S(1)} %get-tuple-element.10.conv_ref, ...), custom_call_target="tpu_custom_call" | custom-call | flops 4194304 | bytes 401408 | tf_op jit(solution)/shard_map/pallas_call | solution.py:420
  12.8 12.3 %all_to_all.10.recv_ref = bf16[32,8,384]{2,1,0:T(8,128)(2,1)S(1)} all-to-all(bf16[32,8,384]{2,1,0:T(8,128)(2,1)S(1)} %shard_map.106), channel_id=1, replica_groups={{31,10,20,3,13,27,6,16,30,9,23,2,12,26,5,19,29,8,22,1,15,25,4,18,28,11,..., dimensions={0} | all-to-all | bytes 393216 | tf_op jit(solution)/shard_map/all_to_all | solution.py:479
  25.1 1.2 %shard_map.107 = (f32[9,32,256]{2,1,0:T(8,128)}, f32[6,32]{1,0:T(8,128)}) custom-call(bf16[32,8,384]{2,1,0:T(8,128)(2,1)S(1)} %all_to_all.10.recv_ref, bf16[128,256]{1,0:T(8,128)(2,1)S(1)} %get-tuple-element.11.proj_rep_ref), custom_call_target="tpu_custom_call" | custom-call | tf_op jit(solution)/shard_map/pallas_call | solution.py:488
Async XLA Ops:
  0.6 7.1 %copy-start.4 = (bf16[3,6,2048]{2,1,0:T(8,128)(2,1)S(1)}, bf16[3,6,2048]{2,1,0:T(8,128)(2,1)}, u32[]{:S(2)}) copy-start(bf16[3,6,2048]{2,1,0:T(8,128)(2,1)} %fold_ref.1) | copy-start | bytes 221188
  0.6 7.0 %copy-start.5 = (bf16[1,1,8,256]{3,2,1,0:T(8,128)(2,1)S(1)}, bf16[1,1,8,256]{3,2,1,0:T(8,128)(2,1)}, u32[]{:S(2)}) copy-start(bf16[1,1,8,256]{3,2,1,0:T(8,128)(2,1)} %conv_ref.1) | copy-start | bytes 12292
  0.7 7.0 %copy-start.6 = (bf16[6,256]{1,0:T(8,128)(2,1)S(1)}, bf16[6,256]{1,0:T(8,128)(2,1)}, u32[]{:S(2)}) copy-start(bf16[6,256]{1,0:T(8,128)(2,1)} %proj_ref.1) | copy-start | bytes 9220
  0.7 7.0 %copy-start.8 = (f32[1,6,1,8]{3,2,1,0:T(1,128)S(1)}, f32[1,6,1,8]{3,2,1,0:T(1,128)}, u32[]{:S(2)}) copy-start(f32[1,6,1,8]{3,2,1,0:T(1,128)} %dec_ref.1) | copy-start | bytes 580
  2.2 5.5 %copy-start = (bf16[1,1,8,2048]{3,2,1,0:T(8,128)(2,1)S(1)}, bf16[1,1,8,2048]{3,2,1,0:T(8,128)(2,1)}, u32[]{:S(2)}) copy-start(bf16[1,1,8,2048]{3,2,1,0:T(8,128)(2,1)} %query_ref.3) | copy-start | bytes 98308
  2.2 5.5 %copy-start.1 = (bf16[1,1,8,2048]{3,2,1,0:T(8,128)(2,1)S(1)}, bf16[1,1,8,2048]{3,2,1,0:T(8,128)(2,1)}, u32[]{:S(2)}) copy-start(bf16[1,1,8,2048]{3,2,1,0:T(8,128)(2,1)} %key_ref.3) | copy-start | bytes 98308
  2.2 5.5 %copy-start.2 = (bf16[1,1,8,2048]{3,2,1,0:T(8,128)(2,1)S(1)}, bf16[1,1,8,2048]{3,2,1,0:T(8,128)(2,1)}, u32[]{:S(2)}) copy-start(bf16[1,1,8,2048]{3,2,1,0:T(8,128)(2,1)} %value_ref.3) | copy-start | bytes 98308
  2.2 5.5 %copy-start.3 = (bf16[1,1,8,2048]{3,2,1,0:T(8,128)(2,1)S(1)}, bf16[1,1,8,2048]{3,2,1,0:T(8,128)(2,1)}, u32[]{:S(2)}) copy-start(bf16[1,1,8,2048]{3,2,1,0:T(8,128)(2,1)} %grad_ref.3) | copy-start | bytes 98308
  2.2 9.8 %all-to-all-start = ((bf16[8,4,8,128]{3,2,1,0:T(8,128)(2,1)}), bf16[8,4,8,128]{3,2,1,0:T(8,128)(2,1)S(1)}, u32[]{:S(2)}, u32[]{:S(2)}) async-start(bf16[8,4,8,128]{3,2,1,0:T(8,128)(2,1)} %shard_map.104), calls=%async_computation | async-start | bytes 131072 | tf_op jit(solution)/shard_map/all_to_all | solution.py:462
  9.0 3.1 %copy-start.7 = (bf16[1,1,8,256]{3,2,1,0:T(8,128)(2,1)S(1)}, bf16[1,1,8,256]{3,2,1,0:T(8,128)(2,1)}, u32[]{:S(2)}) copy-start(bf16[1,1,8,256]{3,2,1,0:T(8,128)(2,1)} %pre_ref.1) | copy-start | bytes 12292

commit v5 on v4

--- a/solution.py
+++ b/solution.py
@@ -241,8 +241,10 @@
     fold_ref,
     dec_ref,
     conv_ref,
+    pre_ref,
     proj_ref,
     row_ref,
+    slope_ref,
     fold_own_ref,
     conv_out_ref,
     proj_rep_ref,
@@ -298,6 +300,24 @@
     )
     row_ref[...] = jnp.where(iota((width, lanes), 0) == mine, vector, 0.0)
     proj_rep_ref[...] = dot(once, proj_ref[...]).astype(HALFWORD)
+    pre_wide = pre_ref[0, 0].astype(FLOAT)
+    act_low = (pre_wide * jax.nn.sigmoid(pre_wide)).astype(HALFWORD)
+    proj_all = dot(spread, proj_ref[...]).astype(HALFWORD)
+    latent_pre = dot(act_low, proj_all, 1, 1)
+    halves = [(levels_one - 1.0) * 1.001 / 2.0 for levels_one in fsq_levels]
+    _, channel, _ = lane_places(width, lanes, span, latents, width)
+    shift = jnp.zeros((width, lanes), FLOAT)
+    slope = jnp.zeros((width, lanes), FLOAT)
+    for index, (levels_one, bins_one, half_width) in enumerate(zip(fsq_levels, fsq_bins, halves)):
+        ratio_one = (0.5 if levels_one % 2.0 == 0.0 else 0.0) / half_width
+        shift_one = 0.5 * math.log((1.0 + ratio_one) / (1.0 - ratio_one))
+        shift = jnp.where(channel == index, shift_one, shift)
+        slope = jnp.where(channel == index, half_width / bins_one, slope)
+    tanh_val = jnp.tanh(latent_pre + shift)
+    slope = slope * (1.0 - tanh_val * tanh_val)
+    slope = jnp.where(inside & (iota((width, lanes), 0) == place), slope, 0.0)
+    vector = jnp.sum(slope, axis=0, keepdims=True)
+    slope_ref[...] = jnp.where(iota((width, lanes), 0) == mine, vector, 0.0)
     for device in range(devices):
         first = device * span
         block = conv_ref[0, 0, :, first // lanes * lanes : first // lanes * lanes + lanes].astype(FLOAT)
@@ -306,11 +326,12 @@
         conv_out_ref[device] = block
 
 
-def column_kernel(seq_order, all_order, recv_ref, fold_ref, row_ref, conv_ref, pre_ref, out_ref):
+def column_kernel(
+    seq_order, chip_order, recv_ref, fold_ref, row_ref, slope_ref, conv_ref, pre_ref, out_ref
+):
     rows, _, width, _ = recv_ref.shape
     devices, _, lanes = conv_ref.shape
     channels = pre_ref.shape[3]
-    images = out_ref.shape[0] // devices
     span = channels // devices
     half = (lanes - span) // 2
     count = rows * width
@@ -328,90 +349,111 @@
     match = iota((width, lanes), 0) == rem(iota((width, lanes), 1), width)
     total = jnp.where(match[None], total.reshape(rows, width, lanes), 0.0)
     share = jnp.sum(total, axis=1) + row_ref[...]
-    high = share.astype(HALFWORD).astype(FLOAT)
     lane = iota((rows, lanes), 1)
-    pair = jnp.where(lane < span + half, high, share - high)
+
+    def pair(value):
+        high = value.astype(HALFWORD).astype(FLOAT)
+        return jnp.where(lane < span + half, high, value - high)
+
+    parts = (pair(share), pair(slope_ref[...]))
     pre = pre_ref[0, 0]
-    for device in range(devices):
-        block = jnp.where(lane < span, conv_ref[device], pair).astype(HALFWORD)
-        for image in range(images):
-            slot = all_order.index(image * devices + device)
-            out_ref[slot, :, :channels] = pre
-            out_ref[slot, :, channels:] = block
-
-
-def final_kernel(all_order, recv_ref, proj_rep_ref, conv_out_ref, proj_out_ref, stage, held, small, sem):
-    sources, width, _ = recv_ref.shape
+    chips = devices // 2
+    for chip in range(chips):
+        blocks = [
+            jnp.where(lane < span, conv_ref[2 * chip + core], parts[core]).astype(HALFWORD)
+            for core in range(2)
+        ]
+        for slot, member in enumerate(chip_order):
+            if member % chips == chip:
+                out_ref[slot, :, :channels] = pre
+                out_ref[slot, :, channels : channels + lanes] = blocks[0]
+                out_ref[slot, :, channels + lanes :] = blocks[1]
+
+
+def final_kernel(
+    chip_order, own_ref, other_ref, proj_rep_ref, conv_out_ref, proj_out_ref, stage, held, small, sem
+):
+    members, width, _ = own_ref.shape
     taps, span, channels = conv_out_ref.shape
     latents = proj_out_ref.shape[0]
     lanes = proj_rep_ref.shape[0]
     devices = channels // span
+    chips = devices // 2
+    sources = 2 * members
     images = sources // devices
     count = sources * width
     mine = lax.axis_index("seq")
     half = latents * width
-
-    slots = [all_order.index(source) for source in range(sources)]
-    pre_wide = jnp.concatenate([recv_ref[slot, :, :channels].astype(FLOAT) for slot in slots], axis=0)
-    tail = jnp.stack([recv_ref[slot, :, channels:].astype(FLOAT) for slot in slots], axis=0)
-    pick = jnp.where(iota((span, lanes), 0) == iota((span, lanes), 1), 1.0, 0.0).astype(HALFWORD)
-    inputs = dot(pick, tail.reshape(count, lanes).astype(HALFWORD), 1, 1)
-    position = iota((8, count), 1)
-    place_x = rem(position, width)
-    place_y = rem(div(position, width), devices)
-    for row_off in (-1, 0, 1):
-        for col_off in (-1, 0, 1):
-            step = row_off * width + col_off
-            window = pltpu.roll(inputs, -step % count, 1) if step else inputs
-            valid = (
-                (place_x + col_off >= 0)
-                & (place_x + col_off < width)
-                & (place_y + row_off >= 0)
-                & (place_y + row_off < devices)
-            )
-            window = jnp.where(valid[None], window.reshape(span // 8, 8, count), 0.0)
-            tap = 3 * row_off + col_off + 4
-            stage[pl.ds(tap * span, span), :] = window.reshape(span, count).astype(HALFWORD)
-    proj_rep = proj_rep_ref[...]
-    sigmoid_v = 0.5 + 0.5 * jnp.tanh(0.5 * pre_wide)
-    act_wide = pre_wide * sigmoid_v
-    act_low = act_wide.astype(HALFWORD)
     lane = iota((width, lanes), 1)
     match = (lane >= span) & (lane < span + half) & (iota((width, lanes), 0) == rem(lane, width))
-    latent_pre = dot(act_low, proj_rep, 1, 1).reshape(sources, width, lanes)
-    shares = tail.reshape(images, devices, width, lanes)
-    latent = jnp.sum(shares, axis=1).reshape(sources, lanes)
-    latent = latent + pltpu.roll(latent, lanes - half, 1)
-    halves = [(levels_one - 1.0) * 1.001 / 2.0 for levels_one in fsq_levels]
-    _, channel, _ = lane_places(width, lanes, span, latents, width)
-    shift = jnp.zeros((width, lanes), FLOAT)
-    slope = jnp.zeros((width, lanes), FLOAT)
-    for index, (levels_one, bins_one, half_width) in enumerate(zip(fsq_levels, fsq_bins, halves)):
-        ratio_one = (0.5 if levels_one % 2.0 == 0.0 else 0.0) / half_width
-        shift_one = 0.5 * math.log((1.0 + ratio_one) / (1.0 - ratio_one))
-        shift = jnp.where(channel == index, shift_one, shift)
-        slope = jnp.where(channel == index, half_width / bins_one, slope)
-    tanh_val = jnp.tanh(latent_pre + shift[None])
-    slope = jnp.where(match, slope, 0.0)[None] * (1.0 - tanh_val * tanh_val)
-    wide = jnp.broadcast_to(latent.reshape(sources, 1, lanes), (sources, width, lanes)) * slope
-    wide = wide.reshape(count, lanes).astype(HALFWORD)
-    act_grad = dot(wide, proj_rep)
-    silu_grad = sigmoid_v + act_wide * (1.0 - sigmoid_v)
-    pre_grad = (act_grad * silu_grad).astype(HALFWORD)
-
-    proj_term = dot(wide, act_low, 0, 0)[span : span + half]
-    proj_term = jnp.sum(proj_term.reshape(latents, width, channels), axis=1)
-    small[...] = pltpu.roll(proj_term, rem(channels - mine * span, channels), 1)[:, :span]
-    copies = [pltpu.make_async_copy(small, proj_out_ref, sem.at[3])]
-    copies[0].start()
-    for part in range(3):
-        rows = pl.ds(3 * part, 3)
-        windows = stage[3 * part * span : 3 * (part + 1) * span, :]
-        held[rows] = dot(windows, pre_grad).reshape(3, span, channels)
-        copies.append(pltpu.make_async_copy(held.at[rows], conv_out_ref.at[rows], sem.at[part]))
-        copies[-1].start()
-    for copy in copies:
-        copy.wait()
+
+    def finish(core):
+        def rows(first, size):
+            tiles = []
+            for source in range(sources):
+                image, place = divmod(source, devices)
+                ref = own_ref if place % 2 == core else other_ref
+                slot = chip_order.index(image * chips + place // 2)
+                tiles.append(ref[slot, :, first : first + size].astype(FLOAT))
+            return jnp.stack(tiles, axis=0)
+
+        tails = [rows(channels, lanes), rows(channels + lanes, lanes)]
+        pick = jnp.where(iota((span, lanes), 0) == iota((span, lanes), 1), 1.0, 0.0)
+        inputs = dot(
+            pick.astype(HALFWORD), tails[core].reshape(count, lanes).astype(HALFWORD), 1, 1
+        )
+        position = iota((8, count), 1)
+        place_x = rem(position, width)
+        place_y = rem(div(position, width), devices)
+        for row_off in (-1, 0, 1):
+            for col_off in (-1, 0, 1):
+                step = row_off * width + col_off
+                window = pltpu.roll(inputs, -step % count, 1) if step else inputs
+                valid = (
+                    (place_x + col_off >= 0)
+                    & (place_x + col_off < width)
+                    & (place_y + row_off >= 0)
+                    & (place_y + row_off < devices)
+                )
+                window = jnp.where(valid[None], window.reshape(span // 8, 8, count), 0.0)
+                tap = 3 * row_off + col_off + 4
+                stage[pl.ds(tap * span, span), :] = window.reshape(span, count).astype(HALFWORD)
+        proj_rep = proj_rep_ref[...]
+        latent, slope = [
+            jnp.sum(tail.reshape(images, devices, width, lanes), axis=1).reshape(sources, lanes)
+            for tail in tails
+        ]
+        latent = latent + pltpu.roll(latent, lanes - half, 1)
+        slope = slope + pltpu.roll(slope, lanes - half, 1)
+        latent_grad = (latent * slope).reshape(sources, 1, lanes)
+        wide = jnp.broadcast_to(latent_grad, (sources, width, lanes))
+        wide = jnp.where(match[None], wide, 0.0).reshape(count, lanes).astype(HALFWORD)
+        act_grad = dot(wide, proj_rep)
+        pre_wide = rows(0, channels).reshape(count, channels)
+        sigmoid_v = 0.5 + 0.5 * jnp.tanh(0.5 * pre_wide)
+        act_wide = pre_wide * sigmoid_v
+        act_low = act_wide.astype(HALFWORD)
+        silu_grad = sigmoid_v + act_wide * (1.0 - sigmoid_v)
+        pre_grad = (act_grad * silu_grad).astype(HALFWORD)
+        proj_term = dot(wide, act_low, 0, 0)[span : span + half]
+        proj_term = jnp.sum(proj_term.reshape(latents, width, channels), axis=1)
+        turn = rem(channels - mine * span, channels)
+        small[...] = pltpu.roll(proj_term, turn, 1)[:, :span]
+        copies = [pltpu.make_async_copy(small, proj_out_ref, sem.at[3])]
+        copies[0].start()
+        for part in range(3):
+            block = pl.ds(3 * part, 3)
+            windows = stage[3 * part * span : 3 * (part + 1) * span, :]
+            held[block] = dot(windows, pre_grad).reshape(3, span, channels)
+            copies.append(
+                pltpu.make_async_copy(held.at[block], conv_out_ref.at[block], sem.at[part])
+            )
+            copies[-1].start()
+        for copy in copies:
+            copy.wait()
+
+    for core in range(2):
+        pl.when(rem(mine, 2) == core)(functools.partial(finish, core))
 
 
 def call(kernel, outs, inputs, in_specs=None, flops=1 << 22):
@@ -446,9 +488,13 @@
     heads = (attn_queries, attn_keys, attn_values, out_grad)
     struct = jax.ShapeDtypeStruct
     members = images * devices
-    stride = 3 * members // 8 + 1
-    seq_order = [(1 - slot) % devices for slot in range(devices)]
-    all_order = [(members - 1 - stride * slot) % members for slot in range(members)]
+    chips = devices // 2
+    seq_order = [(devices // 2 - 1 - slot) % devices for slot in range(devices)]
+    chip_order = [(members // 2 - 1 + slot) % (members // 2) for slot in range(members // 2)]
+    core_groups = [
+        [member // chips * devices + member % chips * 2 + core for member in chip_order]
+        for core in range(2)
+    ]
     columns = [pl.BlockSpec((1, 1, width, split_at), lambda step: (0, 0, 0, 1))] * 4
     rows = [pl.BlockSpec((1, 1, width, split_at), lambda step: (0, 0, 0, 0))] * 4
     whole = pl.BlockSpec(memory_space=pltpu.VMEM)
@@ -460,41 +506,43 @@
         scratch_shapes=[pltpu.VMEM((devices, 4, width, HEAD_DIM), HALFWORD), pltpu.SemaphoreType.DMA, pltpu.SemaphoreType.DMA],
     )(*heads)
     column = lax.all_to_all(packed, "seq", split_axis=0, concat_axis=0, axis_index_groups=[seq_order], tiled=True)
-    row_share, fold_own, conv_blocks, proj_rep = call(
+    row_share, slopes, fold_own, conv_blocks, proj_rep = call(
         local_kernel,
         [
+            struct((width, LANES), FLOAT),
             struct((width, LANES), FLOAT),
             struct((3, LANES, HEAD_DIM), HALFWORD),
             struct((devices, width, LANES), FLOAT),
             struct((LANES, channels), HALFWORD),
         ],
-        (*heads, fold_maps, dec_grad, conv_input, proj_weight),
-        rows + [whole] * 4,
+        (*heads, fold_maps, dec_grad, conv_input, pre_act, proj_weight),
+        rows + [whole] * 5,
     )
     (shared,) = call(
-        functools.partial(column_kernel, seq_order, all_order),
-        [struct((images * devices, width, channels + LANES), HALFWORD)],
-        (column, fold_own, row_share, conv_blocks, pre_act),
+        functools.partial(column_kernel, seq_order, chip_order),
+        [struct((members // 2, width, channels + 2 * LANES), HALFWORD)],
+        (column, fold_own, row_share, slopes, conv_blocks, pre_act),
     )
     spread = lax.all_to_all(
         shared,
         ("dp", "seq"),
         split_axis=0,
         concat_axis=0,
-        axis_index_groups=[all_order],
+        axis_index_groups=core_groups,
         tiled=True,
     )
+    partner = lax.ppermute(spread, "seq", [(one, one ^ 1) for one in range(devices)])
     outs = [struct((9, span, channels), FLOAT), struct((latents, span), FLOAT)]
     conv_out, proj_out = pl.pallas_call(
-        functools.partial(final_kernel, all_order),
+        functools.partial(final_kernel, chip_order),
         out_shape=outs,
-        in_specs=[whole] * 2,
+        in_specs=[whole] * 3,
         out_specs=[pl.BlockSpec(memory_space=pltpu.HBM)] * 2,
         scratch_shapes=[pltpu.VMEM((9 * span, images * devices * width), HALFWORD)]
         + [pltpu.VMEM(one.shape, one.dtype) for one in outs]
         + [pltpu.SemaphoreType.DMA((4,))],
         compiler_params=pltpu.CompilerParams(vmem_limit_bytes=16 << 20),
-    )(spread, proj_rep)
+    )(spread, partner, proj_rep)
     return (jnp.transpose(conv_out, (1, 0, 2)), jnp.transpose(proj_out, (1, 0)))
 
 
@@ -509,7 +557,7 @@
         (conv_input.shape[0], rows, width, heads) == (1, 1, devices, devices)
         and channels // devices % 8 == 0
         and (HALF * 2, width, images * devices % 8) == (queries.shape[3] // HEAD_DIM, 8, 0)
-        and math.gcd(3 * images * devices // 8 + 1, images * devices) == 1
+        and devices % 2 == 0
         and channels // devices + 2 * latents * width == LANES
     )
     if fits and positions * channels * 2 <= 9 * channels * channels * 4:

time: 26.6 us -> 26 us (0.977)
  blocking collectives: 12.3 us -> 10.8 us
  waiting for transfers between devices: 3.06 us -> 3.67 us
  starting transfers between devices: 5.45 us -> 5.82 us
    all_to_all x1, blocking collectives: 12.3 us -> 10.8 us  [gather_plan(): lax.all_to_all(shared, ('dp', 'seq'), split_axis=0, concat_axis=0, axis_i...]
    ppermute x0 -> x1, waiting for transfers between devices: none -> 1.35 us  [gather_plan(): lax.ppermute(spread, 'seq', [(one, one ^ 1) for one in range(devices)])]
    all_to_all x1, waiting for transfers between devices: 3.06 us -> 2.33 us  [gather_plan(): lax.all_to_all(packed, 'seq', split_axis=0, concat_axis=0, axis_index_gro...]
    all_to_all x1, starting transfers between devices: 5.45 us -> 5.82 us  [gather_plan(): lax.all_to_all(packed, 'seq', split_axis=0, concat_axis=0, axis_index_gro...]
  transfers between devices with their start and end apart: 1 -> 2, of which waited for: 1 -> 2; matrix products, arithmetic and copies ran while one was open for 0% -> 0% of each run, Pallas kernels for 5% -> 5%
where the time goes in v5:
time: 26 us; the launch traced here: 25.6 us
  blocking collectives  10.8 us (42%)
  starting transfers between devices  5.82 us (22%)
  Pallas kernels  4.56 us (18%)
  waiting for transfers between devices  3.67 us (14%)
  between operations  0.78 us (3%)
    all_to_all x1, blocking collectives, gather_plan(): lax.all_to_all(shared, ('dp', 'seq'), split_axis=0, concat_axis=0, axis_i...  10.8 us
    all_to_all x1, starting transfers between devices, gather_plan(): lax.all_to_all(packed, 'seq', split_axis=0, concat_axis=0, axis_index_gro...  5.82 us
    all_to_all x1, waiting for transfers between devices, gather_plan(): lax.all_to_all(packed, 'seq', split_axis=0, concat_axis=0, axis_index_gro...  2.33 us
    pallas_call x2, Pallas kernels, call(): pl.pallas_call(kernel, grid=(1,), out_shape=outs, in_specs=in_specs or [w...  1.87 us
    pallas_call x1, Pallas kernels, gather_plan(): pl.pallas_call(functools.partial(pack_kernel, seq_order), out_shape=struc...  1.49 us
    ppermute x1, waiting for transfers between devices, gather_plan(): lax.ppermute(spread, 'seq', [(one, one ^ 1) for one in range(devices)])  1.35 us
    pallas_call x1, Pallas kernels, gather_plan(): pl.pallas_call(functools.partial(final_kernel, chip_order), out_shape=out...  1.2 us
  transfers between devices with their start and end apart: 2, of which 2 were waited for; matrix products, arithmetic and copies ran while one was open for 0% of the time, Pallas kernels for 5%

profile of v5, /device:TPU:0, one launch (start us, length us, event | category | flops | bytes accessed | tf_op | source)
XLA Modules:
  0.0 25.6 jit_solution(6997269581876865308)
XLA Ops:
  0.6 0.0 copy-start.4
  0.6 0.0 copy-start.5
  0.7 0.0 copy-start.6
  0.7 0.0 copy-start.7
  0.7 0.0 copy-start.8
  0.7 1.5 %shard_map.104 = bf16[8,4,8,128]{3,2,1,0:T(8,128)(2,1)} custom-call(bf16[1,1,8,2048]{3,2,1,0:T(8,128)(2,1)} %query_ref.3, bf16[1,1,8,2048]{3,2,1,0:T(8,128)(2,1)} %key_ref.3, bf16[1,1,8,2048]{3,2,1,0:T(8,128)(2,1)} %value_ref.3, bf16[1,1,8,2048]{3,2,1,0:T(8,128)(2,1)} %grad_ref.3), custom_call_target="tpu_custom_call" | custom-call | tf_op jit(solution)/shard_map/pallas_call | solution.py:501
  2.2 0.0 copy-start
  2.2 0.0 copy-start.1
  2.2 0.0 copy-start.2
  2.2 0.0 copy-start.3
  2.2 5.8 %all-to-all-start = ((bf16[8,4,8,128]{3,2,1,0:T(8,128)(2,1)}), bf16[8,4,8,128]{3,2,1,0:T(8,128)(2,1)S(1)}, u32[]{:S(2)}, u32[]{:S(2)}) async-start(bf16[8,4,8,128]{3,2,1,0:T(8,128)(2,1)} %shard_map.104), calls=%async_computation | async-start | bytes 131072 | tf_op jit(solution)/shard_map/all_to_all | solution.py:508
  8.0 0.0 copy-done.4
  8.1 0.0 copy-done.5
  8.1 0.0 copy-done.6
  8.1 0.0 copy-done.7
  8.1 0.0 copy-done.8
  8.1 0.0 copy-done
  8.1 0.0 copy-done.1
  8.1 0.0 copy-done.2
  8.1 0.0 copy-done.3
  8.1 1.2 %shard_map.105 = (f32[8,128]{1,0:T(8,128)S(1)}, f32[8,128]{1,0:T(8,128)S(1)}, bf16[3,128,128]{2,1,0:T(8,128)(2,1)S(1)}, f32[8,8,128]{2,1,0:T(8,128)S(1)}, bf16[128,256]{1,0:T(8,128)(2,1)S(1)}) custom-call(bf16[1,1,8,2048]{3,2,1,0:T(8,128)(2,1)S(1)} %copy-done, bf16[1,1,8,2048]{3,2,1,0:T(8,128)(2,1)S(1)} %copy-done.1, bf16[1,1,8,2048]{3,2,1,0:T(8,128)(2,1)S(1)} %copy-done.2, ...), custom_call_target="tpu_custom_call" | custom-call | flops 4194304 | bytes 421056 | tf_op jit(solution)/shard_map/pallas_call | solution.py:462
  9.3 2.3 %all-to-all-done.recv_ref = bf16[8,4,8,128]{3,2,1,0:T(8,128)(2,1)S(1)} async-done(((bf16[8,4,8,128]{3,2,1,0:T(8,128)(2,1)}), bf16[8,4,8,128]{3,2,1,0:T(8,128)(2,1)S(1)}, u32[]{:S(2)}, u32[]{:S(2)}) %all-to-all-start) | async-done | bytes 65568 | tf_op jit(solution)/shard_map/all_to_all | solution.py:508
  11.6 0.7 %shard_map.106 = bf16[16,8,512]{2,1,0:T(8,128)(2,1)S(1)} custom-call(bf16[8,4,8,128]{3,2,1,0:T(8,128)(2,1)S(1)} %all-to-all-done.recv_ref, bf16[3,128,128]{2,1,0:T(8,128)(2,1)S(1)} %get-tuple-element.9.fold_ref, f32[8,128]{1,0:T(8,128)S(1)} %get-tuple-element.10.row_ref, f32[8,128]{1,0:T(8,128)S(1)} %get-tuple-element.11.slope_ref, ...), custom_call_target="tpu_custom_call" | custom-call | flops 4194304 | bytes 339968 | tf_op jit(solution)/shard_map/pallas_call | solution.py:462
  12.3 10.8 %all_to_all.10.own_ref = bf16[16,8,512]{2,1,0:T(8,128)(2,1)S(1)} all-to-all(bf16[16,8,512]{2,1,0:T(8,128)(2,1)S(1)} %shard_map.106), channel_id=1, replica_groups={{27,0,8,16,24,1,9,17,25,2,10,18,26,3,11,19},{31,4,12,20,28,5,13,21,29,6..., dimensions={0} | all-to-all | bytes 262144 | tf_op jit(solution)/shard_map/all_to_all | solution.py:526
  23.1 0.0 collective-permute-start
  23.1 1.3 %collective-permute-done.other_ref = bf16[16,8,512]{2,1,0:T(8,128)(2,1)S(1)} collective-permute-done((bf16[16,8,512]{2,1,0:T(8,128)(2,1)S(1)}, bf16[16,8,512]{2,1,0:T(8,128)(2,1)S(1)}, u32[]{:S(2)}, u32[]{:S(2)}) %collective-permute-start) | collective-permute-done | bytes 131104 | tf_op jit(solution)/shard_map/ppermute | solution.py:534
  24.4 1.2 %shard_map.107 = (f32[9,32,256]{2,1,0:T(8,128)}, f32[6,32]{1,0:T(8,128)}) custom-call(bf16[16,8,512]{2,1,0:T(8,128)(2,1)S(1)} %all_to_all.10.own_ref, bf16[16,8,512]{2,1,0:T(8,128)(2,1)S(1)} %collective-permute-done.other_ref, bf16[128,256]{1,0:T(8,128)(2,1)S(1)} %get-tuple-element.13.proj_rep_ref), custom_call_target="tpu_custom_call" | custom-call | tf_op jit(solution)/shard_map/pallas_call | solution.py:536
Async XLA Ops:
  0.6 7.4 %copy-start.4 = (bf16[3,6,2048]{2,1,0:T(8,128)(2,1)S(1)}, bf16[3,6,2048]{2,1,0:T(8,128)(2,1)}, u32[]{:S(2)}) copy-start(bf16[3,6,2048]{2,1,0:T(8,128)(2,1)} %fold_ref.1) | copy-start | bytes 221188
  0.6 7.4 %copy-start.5 = (bf16[1,1,8,256]{3,2,1,0:T(8,128)(2,1)S(1)}, bf16[1,1,8,256]{3,2,1,0:T(8,128)(2,1)}, u32[]{:S(2)}) copy-start(bf16[1,1,8,256]{3,2,1,0:T(8,128)(2,1)} %pre_ref.3) | copy-start | bytes 12292
  0.7 7.4 %copy-start.6 = (bf16[1,1,8,256]{3,2,1,0:T(8,128)(2,1)S(1)}, bf16[1,1,8,256]{3,2,1,0:T(8,128)(2,1)}, u32[]{:S(2)}) copy-start(bf16[1,1,8,256]{3,2,1,0:T(8,128)(2,1)} %conv_ref.1) | copy-start | bytes 12292
  0.7 7.4 %copy-start.7 = (bf16[6,256]{1,0:T(8,128)(2,1)S(1)}, bf16[6,256]{1,0:T(8,128)(2,1)}, u32[]{:S(2)}) copy-start(bf16[6,256]{1,0:T(8,128)(2,1)} %proj_ref.1) | copy-start | bytes 9220
  0.7 7.4 %copy-start.8 = (f32[1,6,1,8]{3,2,1,0:T(1,128)S(1)}, f32[1,6,1,8]{3,2,1,0:T(1,128)}, u32[]{:S(2)}) copy-start(f32[1,6,1,8]{3,2,1,0:T(1,128)} %dec_ref.1) | copy-start | bytes 580
  2.2 5.9 %copy-start = (bf16[1,1,8,2048]{3,2,1,0:T(8,128)(2,1)S(1)}, bf16[1,1,8,2048]{3,2,1,0:T(8,128)(2,1)}, u32[]{:S(2)}) copy-start(bf16[1,1,8,2048]{3,2,1,0:T(8,128)(2,1)} %query_ref.3) | copy-start | bytes 98308
  2.2 5.9 %copy-start.1 = (bf16[1,1,8,2048]{3,2,1,0:T(8,128)(2,1)S(1)}, bf16[1,1,8,2048]{3,2,1,0:T(8,128)(2,1)}, u32[]{:S(2)}) copy-start(bf16[1,1,8,2048]{3,2,1,0:T(8,128)(2,1)} %key_ref.3) | copy-start | bytes 98308
  2.2 5.9 %copy-start.2 = (bf16[1,1,8,2048]{3,2,1,0:T(8,128)(2,1)S(1)}, bf16[1,1,8,2048]{3,2,1,0:T(8,128)(2,1)}, u32[]{:S(2)}) copy-start(bf16[1,1,8,2048]{3,2,1,0:T(8,128)(2,1)} %value_ref.3) | copy-start | bytes 98308
  2.2 5.9 %copy-start.3 = (bf16[1,1,8,2048]{3,2,1,0:T(8,128)(2,1)S(1)}, bf16[1,1,8,2048]{3,2,1,0:T(8,128)(2,1)}, u32[]{:S(2)}) copy-start(bf16[1,1,8,2048]{3,2,1,0:T(8,128)(2,1)} %grad_ref.3) | copy-start | bytes 98308
  2.2 9.4 %all-to-all-start = ((bf16[8,4,8,128]{3,2,1,0:T(8,128)(2,1)}), bf16[8,4,8,128]{3,2,1,0:T(8,128)(2,1)S(1)}, u32[]{:S(2)}, u32[]{:S(2)}) async-start(bf16[8,4,8,128]{3,2,1,0:T(8,128)(2,1)} %shard_map.104), calls=%async_computation | async-start | bytes 131072 | tf_op jit(solution)/shard_map/all_to_all | solution.py:508
  23.1 1.3 %collective-permute-start = (bf16[16,8,512]{2,1,0:T(8,128)(2,1)S(1)}, bf16[16,8,512]{2,1,0:T(8,128)(2,1)S(1)}, u32[]{:S(2)}, u32[]{:S(2)}) collective-permute-start(bf16[16,8,512]{2,1,0:T(8,128)(2,1)S(1)} %all_to_all.10.own_ref), channel_id=1, source_target_pairs={{0,4},{4,0},{8,12},{12,8},{16,20},{20,16},{24,28},{28,24},{1,5},{5... | collective-permute-start | bytes 393224 | tf_op jit(solution)/shard_map/ppermute | solution.py:534

commit v6 on v5

--- a/solution.py
+++ b/solution.py
@@ -218,47 +218,70 @@
     return inside, div(offset, width), rem(offset, width)
 
 
-def pack_kernel(order, query_ref, key_ref, value_ref, grad_ref, out_ref, held, sem, out_sem):
-    copies = []
-    for slot, device in enumerate(order):
-        lanes = pl.ds((HALF + device) * HEAD_DIM, HEAD_DIM)
-        for part, ref in enumerate((query_ref, key_ref, value_ref, grad_ref)):
-            copies.append(pltpu.make_async_copy(ref.at[0, 0, :, lanes], held.at[slot, part], sem))
-    for copy in copies:
-        copy.start()
-    for copy in copies:
-        copy.wait()
-    last = pltpu.make_async_copy(held, out_ref, out_sem)
-    last.start()
-    last.wait()
-
-
 def local_kernel(
-    query_ref,
-    key_ref,
-    value_ref,
-    grad_ref,
+    order,
+    query_hbm,
+    key_hbm,
+    value_hbm,
+    grad_hbm,
+    fold_hbm,
+    dec_hbm,
+    conv_hbm,
+    pre_hbm,
+    proj_hbm,
+    packed_ref,
+    row_ref,
+    slope_ref,
+    fold_own_ref,
+    conv_out_ref,
+    proj_rep_ref,
+    pre_out_ref,
+    rows_ref,
     fold_ref,
     dec_ref,
     conv_ref,
     pre_ref,
     proj_ref,
-    row_ref,
-    slope_ref,
-    fold_own_ref,
-    conv_out_ref,
-    proj_rep_ref,
+    sem,
+    pack_sem,
 ):
-    width = query_ref.shape[2]
+    split_at = HALF * HEAD_DIM
+    heads = (query_hbm, key_hbm, value_hbm, grad_hbm)
+    copies = [
+        pltpu.make_async_copy(ref.at[0, 0, :, pl.ds(0, split_at)], rows_ref.at[part], sem)
+        for part, ref in enumerate(heads)
+    ]
+    copies += [
+        pltpu.make_async_copy(source, target, sem)
+        for source, target in (
+            (fold_hbm, fold_ref),
+            (dec_hbm, dec_ref),
+            (conv_hbm, conv_ref),
+            (pre_hbm, pre_ref),
+            (proj_hbm, proj_ref),
+        )
+    ]
+    packs = []
+    for slot, device in enumerate(order):
+        lanes = pl.ds((HALF + device) * HEAD_DIM, HEAD_DIM)
+        for part, ref in enumerate(heads):
+            packs.append(
+                pltpu.make_async_copy(ref.at[0, 0, :, lanes], packed_ref.at[slot, part], pack_sem)
+            )
+    for copy in copies + packs:
+        copy.start()
+    for copy in copies:
+        copy.wait()
+    width = query_hbm.shape[2]
     latents = fold_ref.shape[1]
     devices, _, lanes = conv_out_ref.shape
     span = conv_ref.shape[3] // devices
     mine = lax.axis_index("seq")
 
-    def stacked(ref):
+    def stacked(part):
         return jnp.concatenate(
             [
-                ref[0, 0, :, head * HEAD_DIM : (head + 1) * HEAD_DIM].astype(FLOAT)
+                rows_ref[part, :, head * HEAD_DIM : (head + 1) * HEAD_DIM].astype(FLOAT)
                 for head in range(HALF)
             ],
             axis=0,
@@ -268,7 +291,7 @@
     row, col = iota((count, count), 0), iota((count, count), 1)
     allowed = (div(row, width) == div(col, width)) & (col <= row)
     grads = attend_tile(
-        stacked(query_ref), stacked(key_ref), stacked(value_ref), stacked(grad_ref), allowed
+        stacked(0), stacked(1), stacked(2), stacked(3), allowed
     )
     inside, channel, place = lane_places(width, lanes, span, latents, width)
     lane = iota((lanes, latents), 0)
@@ -276,36 +299,41 @@
     hit = (lane >= span) & (div(spread_at, width) == iota((lanes, latents), 1))
     spread = jnp.where(hit, 1.0, 0.0).astype(HALFWORD)
     once = jnp.where(hit & (lane < span + latents * width), 1.0, 0.0).astype(HALFWORD)
-    split_at = HALF * HEAD_DIM
-    total = jnp.zeros((width, lanes), FLOAT)
+    compact = jnp.zeros((width, latents), FLOAT)
     for part in range(3):
-        maps = dot(spread, fold_ref[part, :, :split_at]).astype(HALFWORD)
         wide = grads[part].astype(FLOAT)
         wide = jnp.concatenate(
             [wide[head * width : (head + 1) * width] for head in range(HALF)], axis=1
         ).astype(HALFWORD)
-        total = total + dot(wide, maps, 1, 1)
+        compact = compact + dot(wide, fold_ref[part, :, :split_at], 1, 1)
         own = fold_ref[part, :, pl.ds(pl.multiple_of(split_at + mine * HEAD_DIM, HEAD_DIM), HEAD_DIM)]
         fold_own_ref[part] = dot(spread, own).astype(HALFWORD)
-    total = jnp.where(inside & (iota((width, lanes), 0) == place), total, 0.0)
+    diagonal = inside & (iota((width, lanes), 0) == place)
+
+    def spread_out(values):
+        result = jnp.zeros((width, lanes), FLOAT)
+        for index in range(latents):
+            result = jnp.where(diagonal & (channel == index), values[:, index : index + 1], result)
+        return result
+
+    total = spread_out(compact)
     decoder = dec_ref[0, :, 0, :]
     column = jnp.where(
         iota((width, lanes), 0) == rem(iota((width, lanes), 1), width), 1.0, 0.0
     )
     decoder = dot(decoder, column, precision=lax.Precision.HIGHEST)
-    _, channel, _ = lane_places(latents, lanes, span, latents, width)
-    keep = (iota((latents, lanes), 1) >= span) & (iota((latents, lanes), 0) == channel)
+    _, owner, _ = lane_places(latents, lanes, span, latents, width)
+    keep = (iota((latents, lanes), 1) >= span) & (iota((latents, lanes), 0) == owner)
     vector = jnp.sum(total, axis=0, keepdims=True) + jnp.sum(
         jnp.where(keep, decoder, 0.0), axis=0, keepdims=True
     )
     row_ref[...] = jnp.where(iota((width, lanes), 0) == mine, vector, 0.0)
     proj_rep_ref[...] = dot(once, proj_ref[...]).astype(HALFWORD)
+    pre_out_ref[...] = pre_ref[...]
     pre_wide = pre_ref[0, 0].astype(FLOAT)
     act_low = (pre_wide * jax.nn.sigmoid(pre_wide)).astype(HALFWORD)
-    proj_all = dot(spread, proj_ref[...]).astype(HALFWORD)
-    latent_pre = dot(act_low, proj_all, 1, 1)
+    latent_pre = spread_out(dot(act_low, proj_ref[...], 1, 1))
     halves = [(levels_one - 1.0) * 1.001 / 2.0 for levels_one in fsq_levels]
-    _, channel, _ = lane_places(width, lanes, span, latents, width)
     shift = jnp.zeros((width, lanes), FLOAT)
     slope = jnp.zeros((width, lanes), FLOAT)
     for index, (levels_one, bins_one, half_width) in enumerate(zip(fsq_levels, fsq_bins, halves)):
@@ -315,7 +343,7 @@
         slope = jnp.where(channel == index, half_width / bins_one, slope)
     tanh_val = jnp.tanh(latent_pre + shift)
     slope = slope * (1.0 - tanh_val * tanh_val)
-    slope = jnp.where(inside & (iota((width, lanes), 0) == place), slope, 0.0)
+    slope = jnp.where(diagonal, slope, 0.0)
     vector = jnp.sum(slope, axis=0, keepdims=True)
     slope_ref[...] = jnp.where(iota((width, lanes), 0) == mine, vector, 0.0)
     for device in range(devices):
@@ -324,6 +352,8 @@
         if first % lanes:
             block = pltpu.roll(block, lanes - first % lanes, 1)
         conv_out_ref[device] = block
+    for copy in packs:
+        copy.wait()
 
 
 def column_kernel(
@@ -496,32 +526,31 @@
         for core in range(2)
     ]
     columns = [pl.BlockSpec((1, 1, width, split_at), lambda step: (0, 0, 0, 1))] * 4
-    rows = [pl.BlockSpec((1, 1, width, split_at), lambda step: (0, 0, 0, 0))] * 4
     whole = pl.BlockSpec(memory_space=pltpu.VMEM)
-    packed = pl.pallas_call(
-        functools.partial(pack_kernel, seq_order),
-        out_shape=struct((devices, 4, width, HEAD_DIM), HALFWORD),
-        in_specs=[pl.BlockSpec(memory_space=pltpu.HBM)] * 4,
-        out_specs=pl.BlockSpec(memory_space=pltpu.HBM),
-        scratch_shapes=[pltpu.VMEM((devices, 4, width, HEAD_DIM), HALFWORD), pltpu.SemaphoreType.DMA, pltpu.SemaphoreType.DMA],
-    )(*heads)
-    column = lax.all_to_all(packed, "seq", split_axis=0, concat_axis=0, axis_index_groups=[seq_order], tiled=True)
-    row_share, slopes, fold_own, conv_blocks, proj_rep = call(
-        local_kernel,
-        [
+    inputs = (*heads, fold_maps, dec_grad, conv_input, pre_act, proj_weight)
+    packed, row_share, slopes, fold_own, conv_blocks, proj_rep, pre_near = pl.pallas_call(
+        functools.partial(local_kernel, seq_order),
+        out_shape=[
+            struct((devices, 4, width, HEAD_DIM), HALFWORD),
             struct((width, LANES), FLOAT),
             struct((width, LANES), FLOAT),
             struct((3, LANES, HEAD_DIM), HALFWORD),
             struct((devices, width, LANES), FLOAT),
             struct((LANES, channels), HALFWORD),
+            struct(pre_act.shape, HALFWORD),
         ],
-        (*heads, fold_maps, dec_grad, conv_input, pre_act, proj_weight),
-        rows + [whole] * 5,
-    )
+        in_specs=[pl.BlockSpec(memory_space=pltpu.HBM)] * len(inputs),
+        out_specs=[whole] * 7,
+        scratch_shapes=[pltpu.VMEM((4, width, split_at), HALFWORD)]
+        + [pltpu.VMEM(one.shape, one.dtype) for one in inputs[4:]]
+        + [pltpu.SemaphoreType.DMA, pltpu.SemaphoreType.DMA],
+        compiler_params=pltpu.CompilerParams(vmem_limit_bytes=16 << 20),
+    )(*[pltpu.with_memory_space_constraint(one, pltpu.HBM) for one in inputs])
+    column = lax.all_to_all(packed, "seq", split_axis=0, concat_axis=0, axis_index_groups=[seq_order], tiled=True)
     (shared,) = call(
         functools.partial(column_kernel, seq_order, chip_order),
         [struct((members // 2, width, channels + 2 * LANES), HALFWORD)],
-        (column, fold_own, row_share, slopes, conv_blocks, pre_act),
+        (column, fold_own, row_share, slopes, conv_blocks, pre_near),
     )
     spread = lax.all_to_all(
         shared,

time: 26 us -> 25.7 us (0.988)
  blocking collectives: 10.8 us -> 19.6 us
  starting transfers between devices: 5.82 us -> 0.01 us
  waiting for transfers between devices: 3.67 us -> 1.35 us
  Pallas kernels: 4.56 us -> 3.86 us
    all_to_all x0 -> x1, blocking collectives: none -> 8.84 us  [gather_plan(): lax.all_to_all(packed, 'seq', split_axis=0, concat_axis=0, axis_index_gro...]
    all_to_all x1 -> x0, starting transfers between devices: 5.82 us -> none  [gather_plan(): lax.all_to_all(packed, 'seq', split_axis=0, concat_axis=0, axis_index_gro...]
    all_to_all x1 -> x0, waiting for transfers between devices: 2.33 us -> none  [gather_plan(): lax.all_to_all(packed, 'seq', split_axis=0, concat_axis=0, axis_index_gro...]
    pallas_call x2 -> x1, Pallas kernels: 1.87 us -> 0.69 us  [call(): pl.pallas_call(kernel, grid=(1,), out_shape=outs, in_specs=in_specs or [w...]
    pallas_call x1, Pallas kernels: 1.49 us -> 1.97 us  [gather_plan(): pl.pallas_call(functools.partial(local_kernel, seq_order), out_shape=[str...]
  transfers between devices with their start and end apart: 2 -> 1, of which waited for: 2 -> 1; matrix products, arithmetic and copies ran while one was open for 0% -> 0% of each run, Pallas kernels for 5% -> 0%
where the time goes in v6:
time: 25.7 us; the launch traced here: 25.5 us
  blocking collectives  19.6 us (76%)
  Pallas kernels  3.86 us (15%)
  waiting for transfers between devices  1.35 us (5%)
  between operations  0.65 us (3%)
    all_to_all x1, blocking collectives, gather_plan(): lax.all_to_all(shared, ('dp', 'seq'), split_axis=0, concat_axis=0, axis_i...  10.8 us
    all_to_all x1, blocking collectives, gather_plan(): lax.all_to_all(packed, 'seq', split_axis=0, concat_axis=0, axis_index_gro...  8.84 us
    pallas_call x1, Pallas kernels, gather_plan(): pl.pallas_call(functools.partial(local_kernel, seq_order), out_shape=[str...  1.97 us
    ppermute x1, waiting for transfers between devices, gather_plan(): lax.ppermute(spread, 'seq', [(one, one ^ 1) for one in range(devices)])  1.35 us
    pallas_call x1, Pallas kernels, gather_plan(): pl.pallas_call(functools.partial(final_kernel, chip_order), out_shape=out...  1.2 us
    pallas_call x1, Pallas kernels, call(): pl.pallas_call(kernel, grid=(1,), out_shape=outs, in_specs=in_specs or [w...  0.69 us
  transfers between devices with their start and end apart: 1, of which 1 were waited for; matrix products, arithmetic and copies ran while one was open for 0% of the time, Pallas kernels for 0%

profile of v6, /device:TPU:0, one launch (start us, length us, event | category | flops | bytes accessed | tf_op | source)
XLA Modules:
  0.0 25.5 jit_solution(12532600122449267949)
XLA Ops:
  0.6 2.0 %shard_map.104 = (bf16[8,4,8,128]{3,2,1,0:T(8,128)(2,1)S(1)}, f32[8,128]{1,0:T(8,128)S(1)}, f32[8,128]{1,0:T(8,128)S(1)}, bf16[3,128,128]{2,1,0:T(8,128)(2,1)S(1...) custom-call(bf16[1,1,8,2048]{3,2,1,0:T(8,128)(2,1)} %query_hbm.1, ...), custom_call_target="tpu_custom_call" | custom-call | tf_op jit(solution)/shard_map/pallas_call | solution.py:531
  2.6 8.8 %all_to_all.10.recv_ref = bf16[8,4,8,128]{3,2,1,0:T(8,128)(2,1)S(1)} all-to-all(bf16[8,4,8,128]{3,2,1,0:T(8,128)(2,1)S(1)} %get-tuple-element.11), channel_id=1, replica_groups={{12,8,4,0,28,24,20,16},{13,9,5,1,29,25,21,17},{14,10,6,2,30,26,22,18},{..., dimensions={0} | all-to-all | bytes 131072 | tf_op jit(solution)/shard_map/all_to_all | solution.py:549
  11.4 0.7 %shard_map.105 = bf16[16,8,512]{2,1,0:T(8,128)(2,1)S(1)} custom-call(bf16[8,4,8,128]{3,2,1,0:T(8,128)(2,1)S(1)} %all_to_all.10.recv_ref, bf16[3,128,128]{2,1,0:T(8,128)(2,1)S(1)} %get-tuple-element.12.fold_ref, f32[8,128]{1,0:T(8,128)S(1)} %get-tuple-element.13.row_ref, f32[8,128]{1,0:T(8,128)S(1)} %get-tuple-element.14.slope_ref, ...), custom_call_target="tpu_custom_call" | custom-call | flops 4194304 | bytes 339968 | tf_op jit(solution)/shard_map/pallas_call | solution.py:492
  12.1 10.8 %all_to_all.11.own_ref = bf16[16,8,512]{2,1,0:T(8,128)(2,1)S(1)} all-to-all(bf16[16,8,512]{2,1,0:T(8,128)(2,1)S(1)} %shard_map.105), channel_id=1, replica_groups={{27,0,8,16,24,1,9,17,25,2,10,18,26,3,11,19},{31,4,12,20,28,5,13,21,29,6..., dimensions={0} | all-to-all | bytes 262144 | tf_op jit(solution)/shard_map/all_to_all | solution.py:555
  22.9 0.0 collective-permute-start
  22.9 1.3 %collective-permute-done.other_ref = bf16[16,8,512]{2,1,0:T(8,128)(2,1)S(1)} collective-permute-done((bf16[16,8,512]{2,1,0:T(8,128)(2,1)S(1)}, bf16[16,8,512]{2,1,0:T(8,128)(2,1)S(1)}, u32[]{:S(2)}, u32[]{:S(2)}) %collective-permute-start) | collective-permute-done | bytes 131104 | tf_op jit(solution)/shard_map/ppermute | solution.py:563
  24.3 1.2 %shard_map.106 = (f32[9,32,256]{2,1,0:T(8,128)}, f32[6,32]{1,0:T(8,128)}) custom-call(bf16[16,8,512]{2,1,0:T(8,128)(2,1)S(1)} %all_to_all.11.own_ref, bf16[16,8,512]{2,1,0:T(8,128)(2,1)S(1)} %collective-permute-done.other_ref, bf16[128,256]{1,0:T(8,128)(2,1)S(1)} %get-tuple-element.17.proj_rep_ref), custom_call_target="tpu_custom_call" | custom-call | tf_op jit(solution)/shard_map/pallas_call | solution.py:565
Async XLA Ops:
  22.9 1.3 %collective-permute-start = (bf16[16,8,512]{2,1,0:T(8,128)(2,1)S(1)}, bf16[16,8,512]{2,1,0:T(8,128)(2,1)S(1)}, u32[]{:S(2)}, u32[]{:S(2)}) collective-permute-start(bf16[16,8,512]{2,1,0:T(8,128)(2,1)S(1)} %all_to_all.11.own_ref), channel_id=1, source_target_pairs={{0,4},{4,0},{8,12},{12,8},{16,20},{20,16},{24,28},{28,24},{1,5},{5... | collective-permute-start | bytes 393224 | tf_op jit(solution)/shard_map/ppermute | solution.py:563

commit v7 on v6

--- a/solution.py
+++ b/solution.py
@@ -465,12 +465,7 @@
         act_low = act_wide.astype(HALFWORD)
         silu_grad = sigmoid_v + act_wide * (1.0 - sigmoid_v)
         pre_grad = (act_grad * silu_grad).astype(HALFWORD)
-        proj_term = dot(wide, act_low, 0, 0)[span : span + half]
-        proj_term = jnp.sum(proj_term.reshape(latents, width, channels), axis=1)
-        turn = rem(channels - mine * span, channels)
-        small[...] = pltpu.roll(proj_term, turn, 1)[:, :span]
-        copies = [pltpu.make_async_copy(small, proj_out_ref, sem.at[3])]
-        copies[0].start()
+        copies = []
         for part in range(3):
             block = pl.ds(3 * part, 3)
             windows = stage[3 * part * span : 3 * (part + 1) * span, :]
@@ -479,6 +474,12 @@
                 pltpu.make_async_copy(held.at[block], conv_out_ref.at[block], sem.at[part])
             )
             copies[-1].start()
+        proj_term = dot(wide, act_low, 0, 0)[span : span + half]
+        proj_term = jnp.sum(proj_term.reshape(latents, width, channels), axis=1)
+        turn = rem(channels - mine * span, channels)
+        small[...] = pltpu.roll(proj_term, turn, 1)[:, :span]
+        copies.append(pltpu.make_async_copy(small, proj_out_ref, sem.at[3]))
+        copies[-1].start()
         for copy in copies:
             copy.wait()
 
@@ -519,8 +520,8 @@
     struct = jax.ShapeDtypeStruct
     members = images * devices
     chips = devices // 2
-    seq_order = [(devices // 2 - 1 - slot) % devices for slot in range(devices)]
-    chip_order = [(members // 2 - 1 + slot) % (members // 2) for slot in range(members // 2)]
+    seq_order = [(devices // 2 + 1 - slot) % devices for slot in range(devices)]
+    chip_order = [(members // 2 - 1 - 3 * slot) % (members // 2) for slot in range(members // 2)]
     core_groups = [
         [member // chips * devices + member % chips * 2 + core for member in chip_order]
         for core in range(2)
@@ -587,6 +588,7 @@
         and channels // devices % 8 == 0
         and (HALF * 2, width, images * devices % 8) == (queries.shape[3] // HEAD_DIM, 8, 0)
         and devices % 2 == 0
+        and math.gcd(3, images * devices // 2) == 1
         and channels // devices + 2 * latents * width == LANES
     )
     if fits and positions * channels * 2 <= 9 * channels * channels * 4:

time: 25.7 us -> 25.6 us (level)
  no operation moved by 1% of the time
where the time goes in v7:
time: 25.6 us; the launch traced here: 25.4 us
  blocking collectives  19.6 us (77%)
  Pallas kernels  3.83 us (15%)
  waiting for transfers between devices  1.35 us (5%)
  between operations  0.65 us (3%)
    all_to_all x1, blocking collectives, gather_plan(): lax.all_to_all(shared, ('dp', 'seq'), split_axis=0, concat_axis=0, axis_i...  10.9 us
    all_to_all x1, blocking collectives, gather_plan(): lax.all_to_all(packed, 'seq', split_axis=0, concat_axis=0, axis_index_gro...  8.66 us
    pallas_call x1, Pallas kernels, gather_plan(): pl.pallas_call(functools.partial(local_kernel, seq_order), out_shape=[str...  1.97 us
    ppermute x1, waiting for transfers between devices, gather_plan(): lax.ppermute(spread, 'seq', [(one, one ^ 1) for one in range(devices)])  1.35 us
    pallas_call x1, Pallas kernels, gather_plan(): pl.pallas_call(functools.partial(final_kernel, chip_order), out_shape=out...  1.17 us
    pallas_call x1, Pallas kernels, call(): pl.pallas_call(kernel, grid=(1,), out_shape=outs, in_specs=in_specs or [w...  0.69 us
  transfers between devices with their start and end apart: 1, of which 1 were waited for; matrix products, arithmetic and copies ran while one was open for 0% of the time, Pallas kernels for 0%

profile of v7, /device:TPU:0, one launch (start us, length us, event | category | flops | bytes accessed | tf_op | source)
XLA Modules:
  0.0 25.4 jit_solution(14409838939240090374)
XLA Ops:
  0.6 2.0 %shard_map.104 = (bf16[8,4,8,128]{3,2,1,0:T(8,128)(2,1)S(1)}, f32[8,128]{1,0:T(8,128)S(1)}, f32[8,128]{1,0:T(8,128)S(1)}, bf16[3,128,128]{2,1,0:T(8,128)(2,1)S(1...) custom-call(bf16[1,1,8,2048]{3,2,1,0:T(8,128)(2,1)} %query_hbm.1, ...), custom_call_target="tpu_custom_call" | custom-call | tf_op jit(solution)/shard_map/pallas_call | solution.py:532
  2.6 8.7 %all_to_all.10.recv_ref = bf16[8,4,8,128]{3,2,1,0:T(8,128)(2,1)S(1)} all-to-all(bf16[8,4,8,128]{3,2,1,0:T(8,128)(2,1)S(1)} %get-tuple-element.11), channel_id=1, replica_groups={{20,16,12,8,4,0,28,24},{21,17,13,9,5,1,29,25},{22,18,14,10,6,2,30,26},{..., dimensions={0} | all-to-all | bytes 131072 | tf_op jit(solution)/shard_map/all_to_all | solution.py:550
  11.3 0.7 %shard_map.105 = bf16[16,8,512]{2,1,0:T(8,128)(2,1)S(1)} custom-call(bf16[8,4,8,128]{3,2,1,0:T(8,128)(2,1)S(1)} %all_to_all.10.recv_ref, bf16[3,128,128]{2,1,0:T(8,128)(2,1)S(1)} %get-tuple-element.12.fold_ref, f32[8,128]{1,0:T(8,128)S(1)} %get-tuple-element.13.row_ref, f32[8,128]{1,0:T(8,128)S(1)} %get-tuple-element.14.slope_ref, ...), custom_call_target="tpu_custom_call" | custom-call | flops 4194304 | bytes 339968 | tf_op jit(solution)/shard_map/pallas_call | solution.py:493
  12.0 10.9 %all_to_all.11.own_ref = bf16[16,8,512]{2,1,0:T(8,128)(2,1)S(1)} all-to-all(bf16[16,8,512]{2,1,0:T(8,128)(2,1)S(1)} %shard_map.105), channel_id=1, replica_groups={{27,3,10,17,24,0,11,18,25,1,8,19,26,2,9,16},{31,7,14,21,28,4,15,22,29,5..., dimensions={0} | all-to-all | bytes 262144 | tf_op jit(solution)/shard_map/all_to_all | solution.py:556
  22.9 0.0 collective-permute-start
  22.9 1.3 %collective-permute-done.other_ref = bf16[16,8,512]{2,1,0:T(8,128)(2,1)S(1)} collective-permute-done((bf16[16,8,512]{2,1,0:T(8,128)(2,1)S(1)}, bf16[16,8,512]{2,1,0:T(8,128)(2,1)S(1)}, u32[]{:S(2)}, u32[]{:S(2)}) %collective-permute-start) | collective-permute-done | bytes 131104 | tf_op jit(solution)/shard_map/ppermute | solution.py:564
  24.2 1.2 %shard_map.106 = (f32[9,32,256]{2,1,0:T(8,128)}, f32[6,32]{1,0:T(8,128)}) custom-call(bf16[16,8,512]{2,1,0:T(8,128)(2,1)S(1)} %all_to_all.11.own_ref, bf16[16,8,512]{2,1,0:T(8,128)(2,1)S(1)} %collective-permute-done.other_ref, bf16[128,256]{1,0:T(8,128)(2,1)S(1)} %get-tuple-element.17.proj_rep_ref), custom_call_target="tpu_custom_call" | custom-call | tf_op jit(solution)/shard_map/pallas_call | solution.py:566
Async XLA Ops:
  22.9 1.3 %collective-permute-start = (bf16[16,8,512]{2,1,0:T(8,128)(2,1)S(1)}, bf16[16,8,512]{2,1,0:T(8,128)(2,1)S(1)}, u32[]{:S(2)}, u32[]{:S(2)}) collective-permute-start(bf16[16,8,512]{2,1,0:T(8,128)(2,1)S(1)} %all_to_all.11.own_ref), channel_id=1, source_target_pairs={{0,4},{4,0},{8,12},{12,8},{16,20},{20,16},{24,28},{28,24},{1,5},{5... | collective-permute-start | bytes 393224 | tf_op jit(solution)/shard_map/ppermute | solution.py:564

commit v8 on v7

--- a/solution.py
+++ b/solution.py
@@ -243,6 +243,7 @@
     pre_ref,
     proj_ref,
     sem,
+    rest_sem,
     pack_sem,
 ):
     split_at = HALF * HEAD_DIM
@@ -252,7 +253,7 @@
         for part, ref in enumerate(heads)
     ]
     copies += [
-        pltpu.make_async_copy(source, target, sem)
+        pltpu.make_async_copy(source, target, rest_sem)
         for source, target in (
             (fold_hbm, fold_ref),
             (dec_hbm, dec_ref),
@@ -270,7 +271,7 @@
             )
     for copy in copies + packs:
         copy.start()
-    for copy in copies:
+    for copy in copies[: len(heads)]:
         copy.wait()
     width = query_hbm.shape[2]
     latents = fold_ref.shape[1]
@@ -293,6 +294,8 @@
     grads = attend_tile(
         stacked(0), stacked(1), stacked(2), stacked(3), allowed
     )
+    for copy in copies[len(heads) :]:
+        copy.wait()
     inside, channel, place = lane_places(width, lanes, span, latents, width)
     lane = iota((lanes, latents), 0)
     spread_at = rem(jnp.maximum(lane - span, 0), latents * width)
@@ -544,7 +547,7 @@
         out_specs=[whole] * 7,
         scratch_shapes=[pltpu.VMEM((4, width, split_at), HALFWORD)]
         + [pltpu.VMEM(one.shape, one.dtype) for one in inputs[4:]]
-        + [pltpu.SemaphoreType.DMA, pltpu.SemaphoreType.DMA],
+        + [pltpu.SemaphoreType.DMA] * 3,
         compiler_params=pltpu.CompilerParams(vmem_limit_bytes=16 << 20),
     )(*[pltpu.with_memory_space_constraint(one, pltpu.HBM) for one in inputs])
     column = lax.all_to_all(packed, "seq", split_axis=0, concat_axis=0, axis_index_groups=[seq_order], tiled=True)

time: 25.6 us -> 25.6 us (level)
  no operation moved by 1% of the time
where the time goes in v8:
time: 25.6 us; the launch traced here: 25.3 us
  blocking collectives  19.6 us (77%)
  Pallas kernels  3.77 us (15%)
  waiting for transfers between devices  1.35 us (5%)
  between operations  0.65 us (3%)
    all_to_all x1, blocking collectives, gather_plan(): lax.all_to_all(shared, ('dp', 'seq'), split_axis=0, concat_axis=0, axis_i...  10.9 us
    all_to_all x1, blocking collectives, gather_plan(): lax.all_to_all(packed, 'seq', split_axis=0, concat_axis=0, axis_index_gro...  8.66 us
    pallas_call x1, Pallas kernels, gather_plan(): pl.pallas_call(functools.partial(local_kernel, seq_order), out_shape=[str...  1.92 us
    ppermute x1, waiting for transfers between devices, gather_plan(): lax.ppermute(spread, 'seq', [(one, one ^ 1) for one in range(devices)])  1.35 us
    pallas_call x1, Pallas kernels, gather_plan(): pl.pallas_call(functools.partial(final_kernel, chip_order), out_shape=out...  1.17 us
    pallas_call x1, Pallas kernels, call(): pl.pallas_call(kernel, grid=(1,), out_shape=outs, in_specs=in_specs or [w...  0.69 us
  transfers between devices with their start and end apart: 1, of which 1 were waited for; matrix products, arithmetic and copies ran while one was open for 0% of the time, Pallas kernels for 0%

profile of v8, /device:TPU:0, one launch (start us, length us, event | category | flops | bytes accessed | tf_op | source)
XLA Modules:
  0.0 25.3 jit_solution(10036027559874215711)
XLA Ops:
  0.6 1.9 %shard_map.104 = (bf16[8,4,8,128]{3,2,1,0:T(8,128)(2,1)S(1)}, f32[8,128]{1,0:T(8,128)S(1)}, f32[8,128]{1,0:T(8,128)S(1)}, bf16[3,128,128]{2,1,0:T(8,128)(2,1)S(1...) custom-call(bf16[1,1,8,2048]{3,2,1,0:T(8,128)(2,1)} %query_hbm.1, ...), custom_call_target="tpu_custom_call" | custom-call | tf_op jit(solution)/shard_map/pallas_call | solution.py:535
  2.6 8.7 %all_to_all.10.recv_ref = bf16[8,4,8,128]{3,2,1,0:T(8,128)(2,1)S(1)} all-to-all(bf16[8,4,8,128]{3,2,1,0:T(8,128)(2,1)S(1)} %get-tuple-element.11), channel_id=1, replica_groups={{20,16,12,8,4,0,28,24},{21,17,13,9,5,1,29,25},{22,18,14,10,6,2,30,26},{..., dimensions={0} | all-to-all | bytes 131072 | tf_op jit(solution)/shard_map/all_to_all | solution.py:553
  11.2 0.7 %shard_map.105 = bf16[16,8,512]{2,1,0:T(8,128)(2,1)S(1)} custom-call(bf16[8,4,8,128]{3,2,1,0:T(8,128)(2,1)S(1)} %all_to_all.10.recv_ref, bf16[3,128,128]{2,1,0:T(8,128)(2,1)S(1)} %get-tuple-element.12.fold_ref, f32[8,128]{1,0:T(8,128)S(1)} %get-tuple-element.13.row_ref, f32[8,128]{1,0:T(8,128)S(1)} %get-tuple-element.14.slope_ref, ...), custom_call_target="tpu_custom_call" | custom-call | flops 4194304 | bytes 339968 | tf_op jit(solution)/shard_map/pallas_call | solution.py:496
  11.9 10.9 %all_to_all.11.own_ref = bf16[16,8,512]{2,1,0:T(8,128)(2,1)S(1)} all-to-all(bf16[16,8,512]{2,1,0:T(8,128)(2,1)S(1)} %shard_map.105), channel_id=1, replica_groups={{27,3,10,17,24,0,11,18,25,1,8,19,26,2,9,16},{31,7,14,21,28,4,15,22,29,5..., dimensions={0} | all-to-all | bytes 262144 | tf_op jit(solution)/shard_map/all_to_all | solution.py:559
  22.8 0.0 collective-permute-start
  22.8 1.3 %collective-permute-done.other_ref = bf16[16,8,512]{2,1,0:T(8,128)(2,1)S(1)} collective-permute-done((bf16[16,8,512]{2,1,0:T(8,128)(2,1)S(1)}, bf16[16,8,512]{2,1,0:T(8,128)(2,1)S(1)}, u32[]{:S(2)}, u32[]{:S(2)}) %collective-permute-start) | collective-permute-done | bytes 131104 | tf_op jit(solution)/shard_map/ppermute | solution.py:567
  24.2 1.2 %shard_map.106 = (f32[9,32,256]{2,1,0:T(8,128)}, f32[6,32]{1,0:T(8,128)}) custom-call(bf16[16,8,512]{2,1,0:T(8,128)(2,1)S(1)} %all_to_all.11.own_ref, bf16[16,8,512]{2,1,0:T(8,128)(2,1)S(1)} %collective-permute-done.other_ref, bf16[128,256]{1,0:T(8,128)(2,1)S(1)} %get-tuple-element.17.proj_rep_ref), custom_call_target="tpu_custom_call" | custom-call | tf_op jit(solution)/shard_map/pallas_call | solution.py:569
Async XLA Ops:
  22.8 1.3 %collective-permute-start = (bf16[16,8,512]{2,1,0:T(8,128)(2,1)S(1)}, bf16[16,8,512]{2,1,0:T(8,128)(2,1)S(1)}, u32[]{:S(2)}, u32[]{:S(2)}) collective-permute-start(bf16[16,8,512]{2,1,0:T(8,128)(2,1)S(1)} %all_to_all.11.own_ref), channel_id=1, source_target_pairs={{0,4},{4,0},{8,12},{12,8},{16,20},{20,16},{24,28},{28,24},{1,5},{5... | collective-permute-start | bytes 393224 | tf_op jit(solution)/shard_map/ppermute | solution.py:567

commit v9 on v8

--- a/solution.py
+++ b/solution.py
@@ -321,10 +321,11 @@
 
     total = spread_out(compact)
     decoder = dec_ref[0, :, 0, :]
-    column = jnp.where(
-        iota((width, lanes), 0) == rem(iota((width, lanes), 1), width), 1.0, 0.0
-    )
-    decoder = dot(decoder, column, precision=lax.Precision.HIGHEST)
+    column = rem(iota((latents, lanes), 1), width)
+    tiled = jnp.zeros((latents, lanes), FLOAT)
+    for index in range(width):
+        tiled = jnp.where(column == index, decoder[:, index : index + 1], tiled)
+    decoder = tiled
     _, owner, _ = lane_places(latents, lanes, span, latents, width)
     keep = (iota((latents, lanes), 1) >= span) & (iota((latents, lanes), 0) == owner)
     vector = jnp.sum(total, axis=0, keepdims=True) + jnp.sum(

time: 25.6 us -> 25.6 us (level)
  no operation moved by 1% of the time
where the time goes in v9:
time: 25.6 us; the launch traced here: 25.3 us
  blocking collectives  19.6 us (77%)
  Pallas kernels  3.78 us (15%)
  waiting for transfers between devices  1.35 us (5%)
  between operations  0.65 us (3%)
    all_to_all x1, blocking collectives, gather_plan(): lax.all_to_all(shared, ('dp', 'seq'), split_axis=0, concat_axis=0, axis_i...  10.9 us
    all_to_all x1, blocking collectives, gather_plan(): lax.all_to_all(packed, 'seq', split_axis=0, concat_axis=0, axis_index_gro...  8.66 us
    pallas_call x1, Pallas kernels, gather_plan(): pl.pallas_call(functools.partial(local_kernel, seq_order), out_shape=[str...  1.92 us
    ppermute x1, waiting for transfers between devices, gather_plan(): lax.ppermute(spread, 'seq', [(one, one ^ 1) for one in range(devices)])  1.35 us
    pallas_call x1, Pallas kernels, gather_plan(): pl.pallas_call(functools.partial(final_kernel, chip_order), out_shape=out...  1.17 us
    pallas_call x1, Pallas kernels, call(): pl.pallas_call(kernel, grid=(1,), out_shape=outs, in_specs=in_specs or [w...  0.69 us
  transfers between devices with their start and end apart: 1, of which 1 were waited for; matrix products, arithmetic and copies ran while one was open for 0% of the time, Pallas kernels for 0%

profile of v9, /device:TPU:0, one launch (start us, length us, event | category | flops | bytes accessed | tf_op | source)
XLA Modules:
  0.0 25.3 jit_solution(9524397133207920536)
XLA Ops:
  0.6 1.9 %shard_map.104 = (bf16[8,4,8,128]{3,2,1,0:T(8,128)(2,1)S(1)}, f32[8,128]{1,0:T(8,128)S(1)}, f32[8,128]{1,0:T(8,128)S(1)}, bf16[3,128,128]{2,1,0:T(8,128)(2,1)S(1...) custom-call(bf16[1,1,8,2048]{3,2,1,0:T(8,128)(2,1)} %query_hbm.1, ...), custom_call_target="tpu_custom_call" | custom-call | tf_op jit(solution)/shard_map/pallas_call | solution.py:536
  2.6 8.7 %all_to_all.10.recv_ref = bf16[8,4,8,128]{3,2,1,0:T(8,128)(2,1)S(1)} all-to-all(bf16[8,4,8,128]{3,2,1,0:T(8,128)(2,1)S(1)} %get-tuple-element.11), channel_id=1, replica_groups={{20,16,12,8,4,0,28,24},{21,17,13,9,5,1,29,25},{22,18,14,10,6,2,30,26},{..., dimensions={0} | all-to-all | bytes 131072 | tf_op jit(solution)/shard_map/all_to_all | solution.py:554
  11.2 0.7 %shard_map.105 = bf16[16,8,512]{2,1,0:T(8,128)(2,1)S(1)} custom-call(bf16[8,4,8,128]{3,2,1,0:T(8,128)(2,1)S(1)} %all_to_all.10.recv_ref, bf16[3,128,128]{2,1,0:T(8,128)(2,1)S(1)} %get-tuple-element.12.fold_ref, f32[8,128]{1,0:T(8,128)S(1)} %get-tuple-element.13.row_ref, f32[8,128]{1,0:T(8,128)S(1)} %get-tuple-element.14.slope_ref, ...), custom_call_target="tpu_custom_call" | custom-call | flops 4194304 | bytes 339968 | tf_op jit(solution)/shard_map/pallas_call | solution.py:497
  11.9 10.9 %all_to_all.11.own_ref = bf16[16,8,512]{2,1,0:T(8,128)(2,1)S(1)} all-to-all(bf16[16,8,512]{2,1,0:T(8,128)(2,1)S(1)} %shard_map.105), channel_id=1, replica_groups={{27,3,10,17,24,0,11,18,25,1,8,19,26,2,9,16},{31,7,14,21,28,4,15,22,29,5..., dimensions={0} | all-to-all | bytes 262144 | tf_op jit(solution)/shard_map/all_to_all | solution.py:560
  22.8 0.0 collective-permute-start
  22.8 1.3 %collective-permute-done.other_ref = bf16[16,8,512]{2,1,0:T(8,128)(2,1)S(1)} collective-permute-done((bf16[16,8,512]{2,1,0:T(8,128)(2,1)S(1)}, bf16[16,8,512]{2,1,0:T(8,128)(2,1)S(1)}, u32[]{:S(2)}, u32[]{:S(2)}) %collective-permute-start) | collective-permute-done | bytes 131104 | tf_op jit(solution)/shard_map/ppermute | solution.py:568
  24.2 1.2 %shard_map.106 = (f32[9,32,256]{2,1,0:T(8,128)}, f32[6,32]{1,0:T(8,128)}) custom-call(bf16[16,8,512]{2,1,0:T(8,128)(2,1)S(1)} %all_to_all.11.own_ref, bf16[16,8,512]{2,1,0:T(8,128)(2,1)S(1)} %collective-permute-done.other_ref, bf16[128,256]{1,0:T(8,128)(2,1)S(1)} %get-tuple-element.17.proj_rep_ref), custom_call_target="tpu_custom_call" | custom-call | tf_op jit(solution)/shard_map/pallas_call | solution.py:570
Async XLA Ops:
  22.8 1.3 %collective-permute-start = (bf16[16,8,512]{2,1,0:T(8,128)(2,1)S(1)}, bf16[16,8,512]{2,1,0:T(8,128)(2,1)S(1)}, u32[]{:S(2)}, u32[]{:S(2)}) collective-permute-start(bf16[16,8,512]{2,1,0:T(8,128)(2,1)S(1)} %all_to_all.11.own_ref), channel_id=1, source_target_pairs={{0,4},{4,0},{8,12},{12,8},{16,20},{20,16},{24,28},{28,24},{1,5},{5... | collective-permute-start | bytes 393224 | tf_op jit(solution)/shard_map/ppermute | solution.py:568
